TPU v7x, 256 devices: a whole 4x4x8 slice. The times are simulated.
256 devices in a mesh: sec: 16 (over x, z_lo, core), ty: 4 (over y), tx: 4 (over z_hi).
Axes of the slice: x: 4, y: 4, z: 8 (z_hi: 4, z_lo: 2; z = z_hi * 2 + z_lo), core: 2. Of those that a mesh axis runs over, the one named last changes fastest.
Arguments:
- descriptors: bfloat16 [16, 4, 4, 1024, 128], P('sec', 'ty', 'tx'), may hold values from -4 to 4, as said below
- positions: bfloat16 [16, 4, 4, 2, 1024], P('sec', 'ty', 'tx'), may hold values from -1 to 1
- vertex_ids: int32 [16, 4, 4, 1024], P('sec', 'ty', 'tx'), may hold values from 0 to 262143, as said below
- candidate_blocks: int32 [16, 4, 4, 32], P('sec', 'ty', 'tx'), may hold values from 0 to 127, as said below
- candidate_count: int32 [16, 4, 4], P('sec', 'ty', 'tx'), may hold values from 8 to 32, as said below
- displacement: float32 [16, 2, 512, 512], P('sec', None, 'ty', 'tx'), may hold values from -3 to 3
- stiffness: float32 [16, 512, 512], P('sec', 'ty', 'tx'), may hold values from 0.25 to 4
Outputs:
- relaxed: float32 [16, 2, 512, 512], P('sec', None, 'ty', 'tx')
Inputs may be any that keep to these rules, and one draw needn't show every extreme that they name: `descriptors`: descriptor entries stay within the range. `candidate_blocks`: A list names distinct blocks tile * 8 + j of the next section; among its live entries at most 4 blocks come from any one tile, and some list has 4 live blocks of one tile. `candidate_count`: some tile has all 32 entries live. `vertex_ids`: ids follow the vertex numbering of the steps, anywhere in the section.
All inputs are finite; a program needn't handle non-finite values.
Results may differ from a plain program's by a relative error of at most 0.0019.
Values may be sent and summed in bfloat16 or wider, within the bound.
A program may use at most 192 MiB of HBM per device.

v0:
```python
import jax
import jax.numpy as jnp
from jax import lax
from jax.sharding import PartitionSpec as P

BLK = 128
CAND = 32
ITERS = 4
NB = 8


spring_sec = 0.5
spring_match = 1.0
relax_rate = 0.8


def passed_along(value, axis, by):
    devices = lax.axis_size(axis)
    pairs = [(i, i + by) for i in range(devices) if 0 <= i + by < devices]
    return lax.ppermute(value, axis, pairs)


def extended(value, sides, width):
    for axis, dim in sides:
        devices, length = (lax.axis_size(axis), value.shape[dim])
        up = [(i, (i + 1) % devices) for i in range(devices - 1)]
        down = [(j, i) for i, j in up]
        last = lax.slice_in_dim(value, length - width, length, axis=dim)
        initial = lax.slice_in_dim(value, 0, width, axis=dim)
        before = lax.ppermute(last, axis, up)
        after = lax.ppermute(initial, axis, down)
        value = jnp.concatenate([before, value, after], axis=dim)
    return value


def relax_step(moving, padded, lower_sec, upper_sec, gains, pulled, matched, linked):
    laplace = (
        padded[:, 2:, 1:-1]
        + padded[:, :-2, 1:-1]
        + padded[:, 1:-1, 2:]
        + padded[:, 1:-1, :-2]
        - 4.0 * moving
    )
    spring_force = (
        gains * laplace
        + spring_sec * (lower_sec + upper_sec - linked * moving)
        + spring_match * (pulled - matched * moving)
    )
    diagonal = 4.0 * gains + spring_sec * linked + spring_match * matched
    return moving + relax_rate * spring_force / diagonal


def split_columns(point_values, col_of, mesh_side):
    high_part = point_values.astype(jnp.bfloat16).astype(jnp.float32)
    remain = point_values - high_part
    middle_part = remain.astype(jnp.bfloat16).astype(jnp.float32)
    low_part = (remain - middle_part).astype(jnp.bfloat16).astype(jnp.float32)
    stacked = jnp.stack([high_part, middle_part, low_part], axis=1)
    column_pick = (col_of[:, None] == jnp.arange(mesh_side)[None, :]).astype(jnp.float32)
    weighted = stacked[:, :, :, None] * column_pick[:, None, None, :]
    return weighted.astype(jnp.bfloat16).reshape(point_values.shape[0], 9 * mesh_side)


def row_sums(row_pick, weighted, mesh_side):
    summed = jnp.einsum("ir,ic->rc", row_pick, weighted, preferred_element_type=jnp.float32)
    return jnp.sum(summed.reshape(row_pick.shape[1], 3, 3, mesh_side), axis=1)


def per_device(
    descriptors, positions, vertex_ids, candidate_blocks, candidate_count, displacement, stiffness
):
    queries = descriptors[0, 0, 0]
    point_total = queries.shape[0]
    feature_width = queries.shape[1]
    own_place = positions[0, 0, 0].astype(jnp.float32)
    tile_count = lax.axis_size("ty") * lax.axis_size("tx")
    sections = lax.axis_size("sec")
    sec_index = lax.axis_index("sec")
    score_factor = 16.0 / feature_width
    key_blocks = queries.reshape(NB, BLK, feature_width)
    place_blocks = positions[0, 0, 0].reshape(2, NB, BLK).transpose(1, 0, 2)
    next_keys, next_place = passed_along((key_blocks, place_blocks), "sec", -1)
    block_list = candidate_blocks[0, 0, 0]
    is_valid = jnp.arange(CAND) < candidate_count[0, 0, 0]
    wanted = jnp.any(
        (block_list[:, None] == jnp.arange(tile_count * NB)[None, :]) & is_valid[:, None], axis=0
    )
    row_top = jnp.full((point_total,), -1e30, jnp.float32)
    piece_keys = lax.all_gather(next_keys, ("ty", "tx"), axis=0, tiled=True)
    piece_place = lax.all_gather(next_place, ("ty", "tx"), axis=0, tiled=True)
    block_total = piece_keys.shape[0]
    key_rows = piece_keys.reshape(block_total * BLK, feature_width)
    key_live = jnp.repeat(wanted, BLK)
    scores = jnp.dot(queries, key_rows.T, preferred_element_type=jnp.float32) * score_factor
    masked = jnp.where(key_live[None, :], scores, -1e30)
    new_top = jnp.maximum(row_top, jnp.max(masked, axis=1))
    weights = jnp.where(key_live[None, :], jnp.exp(masked - new_top[:, None]), 0.0)
    key_place = piece_place.transpose(1, 0, 2).reshape(2, block_total * BLK).astype(jnp.float32)
    summed = jnp.einsum("ck,qk->cq", key_place, weights, precision=lax.Precision.HIGHEST)
    row_top, denominator, summed = (new_top, jnp.sum(weights, axis=1), summed)
    target = summed / denominator[None, :]
    has_next = (sec_index < sections - 1).astype(jnp.float32)
    pull_vec = (target - own_place) * has_next
    values = jnp.concatenate([pull_vec, jnp.broadcast_to(has_next, (1, point_total))], axis=0)
    vertex = vertex_ids[0, 0, 0]
    mesh_side = displacement.shape[3]
    row_of = vertex // mesh_side
    weighted = split_columns(values.T, vertex % mesh_side, mesh_side)
    row_pick = (
        row_of[:, None] == jnp.arange(mesh_side * lax.axis_size(("ty", "tx")))[None, :]
    ).astype(jnp.bfloat16)
    owned = lax.psum_scatter(
        row_sums(row_pick, weighted, mesh_side), ("ty", "tx"), scatter_dimension=0, tiled=True
    )
    pulled = owned[:, 0:2, :].transpose(1, 0, 2)
    matched = owned[:, 2, :]
    linked = (sec_index > 0).astype(jnp.float32) + has_next
    moving = displacement[0]
    gains = stiffness[0]
    for sweep in range(ITERS):
        padded = extended(moving, (("ty", 1), ("tx", 2)), 1)
        lower_sec = passed_along(moving, "sec", 1)
        upper_sec = passed_along(moving, "sec", -1)
        moving = relax_step(moving, padded, lower_sec, upper_sec, gains, pulled, matched, linked)
    return moving[None]


def solution(mesh):
    in_specs = (
        P("sec", "ty", "tx", None, None),
        P("sec", "ty", "tx", None, None),
        P("sec", "ty", "tx", None),
        P("sec", "ty", "tx", None),
        P("sec", "ty", "tx"),
        P("sec", None, "ty", "tx"),
        P("sec", "ty", "tx"),
    )
    out_specs = P("sec", None, "ty", "tx")
    return jax.shard_map(
        per_device, mesh=mesh, in_specs=in_specs, out_specs=out_specs, check_vma=False
    )
```

profile of v0, /device:TPU:4, one launch (start us, length us, event | category | flops | bytes accessed | tf_op | source)
XLA Modules:
  0.0 379.9 jit_solution(17649442033626847453)
XLA Ops:
  6.5 3.2 collective-permute-start.6
  9.8 4.2 %collective-permute-done.6 = bf16[8,128,128]{2,1,0:T(8,128)(2,1)S(1)} collective-permute-done((bf16[8,128,128]{2,1,0:T(8,128)(2,1)}, bf16[8,128,128]{2,1,0:T(8,128)(2,1)S(1)}, u32[]{:S(2)}, u32[]{:S(2)}) %collective-permute-start.6) | collective-permute-done | bytes 262176 | tf_op jit(solution)/shard_map/ppermute | solution.py:20
  14.0 0.7 copy-done.2
  14.7 0.0 all-gather.2.cloned.1.call-update
  14.7 0.0 reduce-scatter.2.cloned.1.call-start
  14.7 0.7 copy.16
  15.4 4.6 %collective-permute-start.7 = (bf16[8,2,128]{2,0,1:T(8,128)(2,1)S(1)}, bf16[8,2,128]{2,0,1:T(8,128)(2,1)S(1)}, u32[]{:S(2)}, u32[]{:S(2)}) collective-permute-start(bf16[8,2,128]{2,0,1:T(8,128)(2,1)S(1)} %bitcast.112), channel_id=1, source_target_pairs={{16,0},{32,16},{48,32},{64,48},{80,64},{96,80},{112,96},{128,112},... | collective-permute-start | bytes 12296 | tf_op jit(solution)/shard_map/ppermute | solution.py:20
  20.7 0.7 fusion.72
  21.4 0.7 add_select_fusion
  22.1 0.1 broadcast_bitcast_fusion
  22.2 0.1 fusion.23
  22.3 49.2 %all_gather.7 = bf16[128,2,128]{2,0,1:T(8,128)(2,1)S(1)} all-gather(bf16[8,2,128]{2,0,1:T(8,128)(2,1)S(1)} %collective-permute-done.7), channel_id=1, replica_groups=mesh['sec'=16,'ty'=4,'tx'=4] {'ty','tx'}, dimensions={0}, use_global_device_ids=true | all-gather | bytes 69632 | tf_op jit(solution)/shard_map/all_gather | solution.py:90
  71.4 21.7 %all-gather.2.cloned.1.call-done = bf16[128,128,128]{2,1,0:T(8,128)(2,1)} async-done(((bf16[8,128,128]{2,1,0:T(8,128)(2,1)}), bf16[128,128,128]{2,1,0:T(8,128)(2,1)}) %all-gather.2.cloned.1.call-update) | async-done | bytes 4194320 | tf_op jit(solution)/shard_map/all_gather | solution.py:89
  93.2 26.5 %fusion = (f32[1024]{0:T(1024)S(1)}, f32[1024,16384]{1,0:T(8,128)}) fusion(pred[16384]{0:T(1024)(128)(4,1)S(1)} %broadcast_bitcast_fusion, bf16[16384,128]{1,0:T(8,128)(2,1)} %bitcast.98, bf16[1,1,1,1024,128]{4,3,2,1,0:T(8,128)(2,1)} %param.7), kind=kOutput, calls=%fused_computation.2 | convolution fusion | flops 4345297920 | bytes 71585792 | tf_op jit(solution)/shard_map/dot_general | solution.py:94
  119.7 23.2 %fusion.1 = f32[1024]{0:T(1024)S(1)} fusion(f32[1024,16384]{1,0:T(8,128)} %get-tuple-element.26, f32[1024]{0:T(1024)S(1)} %broadcast_maximum_fusion, pred[16384]{0:T(1024)(128)(4,1)S(1)} %broadcast_bitcast_fusion), kind=kLoop, calls=%fused_computation.3 | loop fusion | flops 83885056 | bytes 67133440 | tf_op jit(solution)/shard_map/reduce_sum | solution.py:100
  142.9 0.0 copy-start.1
  142.9 0.0 copy-start
  142.9 47.5 %fusion.22 = f32[2,1024]{1,0:T(2,128)S(1)} fusion(f32[1024,16384]{1,0:T(8,128)} %get-tuple-element.26, f32[1024]{0:T(1024)S(1)} %broadcast_maximum_fusion, pred[16384]{0:T(1024)(128)(4,1)S(1)} %broadcast_bitcast_fusion, bf16[1,2,128,128]{3,2,1,0:T(8,128)(2,1)S(1)} %bitcast.109, bf16[1,1,1,2,1024]{4,3,2,1,0:T(2,128)(2,1)S(1)} %copy-done.3, ...), kind=kOutput, calls=%fused_computation.22 | convolution fusion | flops 469770240 | bytes 67211264 | tf_op jit(solution)/shard_map/ck,qk->cq/dot_general | solution.py:99
  190.5 7.9 %fusion.12 = f32[2048,3,128]{2,0,1:T(8,128)} fusion(s32[1024]{0:T(1024)S(1)} %get-tuple-element.24, f32[1024,128]{0,1:T(8,128)S(1)} %fusion.23, f32[1024,3,3]{0,2,1:T(4,128)S(1)} %pad_maximum_fusion.36), kind=kOutput, calls=%fused_computation.15 | convolution fusion | flops 4837867520 | bytes 3710976 | tf_op jit(solution)/shard_map/ir,ic->rc/dot_general | solution.py:65
  198.4 0.0 reduce-scatter.2.cloned.1.call-update
  198.5 1.3 collective-permute-start
  199.8 4.5 %collective-permute-start.1 = (f32[2,1,128]{2,1,0:T(1,128)S(1)}, f32[2,1,128]{2,1,0:T(1,128)S(1)}, u32[]{:S(2)}, u32[]{:S(2)}) collective-permute-start(f32[2,1,128]{2,1,0:T(1,128)S(1)} %get-tuple-element.19), channel_id=1, source_target_pairs={{0,4},{4,8},{8,12},{1,5},{5,9},{9,13},{2,6},{6,10},{10,14},{3,7},{... | collective-permute-start | bytes 3080 | tf_op jit(solution)/shard_map/ppermute | solution.py:30
  204.3 1.9 collective-permute-start.4
  206.2 5.0 %collective-permute-start.5 = (f32[2,128,128]{2,1,0:T(8,128)S(1)}, f32[2,128,128]{2,1,0:T(8,128)S(1)}, u32[]{:S(2)}, u32[]{:S(2)}) collective-permute-start(f32[2,128,128]{2,1,0:T(8,128)S(1)} %bitcast.105), channel_id=1, source_target_pairs={{16,0},{32,16},{48,32},{64,48},{80,64},{96,80},{112,96},{128,112},... | collective-permute-start | bytes 393224 | tf_op jit(solution)/shard_map/ppermute | solution.py:20
  211.3 0.0 collective-permute-done
  211.3 0.0 collective-permute-done.1
  211.3 0.1 fusion.83
  211.4 1.3 collective-permute-start.2
  212.7 7.1 %collective-permute-start.3 = (f32[2,130,1]{2,1,0:T(8,128)S(1)}, f32[2,130,1]{2,1,0:T(8,128)S(1)}, u32[]{:S(2)}, u32[]{:S(2)}) collective-permute-start(f32[2,130,1]{2,1,0:T(8,128)S(1)} %get-tuple-element.12), channel_id=1, source_target_pairs={{0,1},{1,2},{2,3},{4,5},{5,6},{6,7},{8,9},{9,10},{10,11},{12,13},{... | collective-permute-start | bytes 3128 | tf_op jit(solution)/shard_map/ppermute | solution.py:30
  219.8 76.1 %reduce-scatter.2.cloned.1.call-done = f32[128,3,128]{2,0,1:T(8,128)} async-done(((f32[2048,3,128]{2,0,1:T(8,128)}), f32[128,3,128]{2,0,1:T(8,128)}) %reduce-scatter.2.cloned.1.call-update) | async-done | bytes 196624 | tf_op jit(solution)/shard_map/reduce_scatter | solution.py:112
  295.9 0.8 fusion.69
  296.8 0.8 slice_bitcast_fusion.1
  297.6 0.0 collective-permute-done.4
  297.7 1.1 fusion.63
  298.8 1.3 collective-permute-start.8
  300.1 4.5 %collective-permute-start.9 = (f32[2,1,128]{2,1,0:T(1,128)S(1)}, f32[2,1,128]{2,1,0:T(1,128)S(1)}, u32[]{:S(2)}, u32[]{:S(2)}) collective-permute-start(f32[2,1,128]{2,1,0:T(1,128)S(1)} %get-tuple-element.17), channel_id=1, source_target_pairs={{0,4},{4,8},{8,12},{1,5},{5,9},{9,13},{2,6},{6,10},{10,14},{3,7},{... | collective-permute-start | bytes 3080 | tf_op jit(solution)/shard_map/ppermute | solution.py:30
  304.6 1.9 collective-permute-start.12
  306.6 4.5 %collective-permute-start.13 = (f32[2,128,128]{2,1,0:T(8,128)S(1)}, f32[2,128,128]{2,1,0:T(8,128)S(1)}, u32[]{:S(2)}, u32[]{:S(2)}) collective-permute-start(f32[2,128,128]{2,1,0:T(8,128)S(1)} %fusion.63), channel_id=1, source_target_pairs={{16,0},{32,16},{48,32},{64,48},{80,64},{96,80},{112,96},{128,112},... | collective-permute-start | bytes 393224 | tf_op jit(solution)/shard_map/ppermute | solution.py:20
  311.1 0.0 collective-permute-done.8
  311.2 0.1 fusion.82
  311.3 1.3 collective-permute-start.10
  312.6 5.5 %collective-permute-start.11 = (f32[2,130,1]{2,1,0:T(8,128)S(1)}, f32[2,130,1]{2,1,0:T(8,128)S(1)}, u32[]{:S(2)}, u32[]{:S(2)}) collective-permute-start(f32[2,130,1]{2,1,0:T(8,128)S(1)} %get-tuple-element.10), channel_id=1, source_target_pairs={{0,1},{1,2},{2,3},{4,5},{5,6},{6,7},{8,9},{9,10},{10,11},{12,13},{... | collective-permute-start | bytes 3128 | tf_op jit(solution)/shard_map/ppermute | solution.py:30
  318.0 3.4 collective-permute-done.10
  321.4 1.1 fusion.53
  322.6 1.3 collective-permute-start.14
  323.9 4.5 %collective-permute-start.15 = (f32[2,1,128]{2,1,0:T(1,128)S(1)}, f32[2,1,128]{2,1,0:T(1,128)S(1)}, u32[]{:S(2)}, u32[]{:S(2)}) collective-permute-start(f32[2,1,128]{2,1,0:T(1,128)S(1)} %get-tuple-element.15), channel_id=1, source_target_pairs={{0,4},{4,8},{8,12},{1,5},{5,9},{9,13},{2,6},{6,10},{10,14},{3,7},{... | collective-permute-start | bytes 3080 | tf_op jit(solution)/shard_map/ppermute | solution.py:30
  328.4 1.9 collective-permute-start.18
  330.3 4.5 %collective-permute-start.19 = (f32[2,128,128]{2,1,0:T(8,128)S(1)}, f32[2,128,128]{2,1,0:T(8,128)S(1)}, u32[]{:S(2)}, u32[]{:S(2)}) collective-permute-start(f32[2,128,128]{2,1,0:T(8,128)S(1)} %fusion.53), channel_id=1, source_target_pairs={{16,0},{32,16},{48,32},{64,48},{80,64},{96,80},{112,96},{128,112},... | collective-permute-start | bytes 393224 | tf_op jit(solution)/shard_map/ppermute | solution.py:20
  334.9 0.0 collective-permute-done.15
  334.9 0.1 fusion.81
  335.0 1.3 collective-permute-start.16
  336.3 5.7 %collective-permute-start.17 = (f32[2,130,1]{2,1,0:T(8,128)S(1)}, f32[2,130,1]{2,1,0:T(8,128)S(1)}, u32[]{:S(2)}, u32[]{:S(2)}) collective-permute-start(f32[2,130,1]{2,1,0:T(8,128)S(1)} %get-tuple-element.8), channel_id=1, source_target_pairs={{0,1},{1,2},{2,3},{4,5},{5,6},{6,7},{8,9},{9,10},{10,11},{12,13},{... | collective-permute-start | bytes 3128 | tf_op jit(solution)/shard_map/ppermute | solution.py:30
  342.1 4.3 %collective-permute-done.16 = f32[2,130,1]{2,1,0:T(8,128)S(1)} collective-permute-done((f32[2,130,1]{2,1,0:T(8,128)S(1)}, f32[2,130,1]{2,1,0:T(8,128)S(1)}, u32[]{:S(2)}, u32[]{:S(2)}) %collective-permute-start.16) | collective-permute-done | bytes 1072 | tf_op jit(solution)/shard_map/ppermute | solution.py:31
  346.4 0.0 collective-permute-done.19
  346.4 1.1 fusion.43
  347.5 1.3 collective-permute-start.20
  348.8 4.5 %collective-permute-start.21 = (f32[2,1,128]{2,1,0:T(1,128)S(1)}, f32[2,1,128]{2,1,0:T(1,128)S(1)}, u32[]{:S(2)}, u32[]{:S(2)}) collective-permute-start(f32[2,1,128]{2,1,0:T(1,128)S(1)} %get-tuple-element.13), channel_id=1, source_target_pairs={{0,4},{4,8},{8,12},{1,5},{5,9},{9,13},{2,6},{6,10},{10,14},{3,7},{... | collective-permute-start | bytes 3080 | tf_op jit(solution)/shard_map/ppermute | solution.py:30
  353.4 1.9 collective-permute-start.24
  355.3 4.5 %collective-permute-start.25 = (f32[2,128,128]{2,1,0:T(8,128)S(1)}, f32[2,128,128]{2,1,0:T(8,128)S(1)}, u32[]{:S(2)}, u32[]{:S(2)}) collective-permute-start(f32[2,128,128]{2,1,0:T(8,128)S(1)} %fusion.43), channel_id=1, source_target_pairs={{16,0},{32,16},{48,32},{64,48},{80,64},{96,80},{112,96},{128,112},... | collective-permute-start | bytes 393224 | tf_op jit(solution)/shard_map/ppermute | solution.py:20
  359.9 0.1 fusion.80
  360.0 1.3 collective-permute-start.22
  361.3 6.6 %collective-permute-start.23 = (f32[2,130,1]{2,1,0:T(8,128)S(1)}, f32[2,130,1]{2,1,0:T(8,128)S(1)}, u32[]{:S(2)}, u32[]{:S(2)}) collective-permute-start(f32[2,130,1]{2,1,0:T(8,128)S(1)} %get-tuple-element.6), channel_id=1, source_target_pairs={{0,1},{1,2},{2,3},{4,5},{5,6},{6,7},{8,9},{9,10},{10,11},{12,13},{... | collective-permute-start | bytes 3128 | tf_op jit(solution)/shard_map/ppermute | solution.py:30
  367.9 3.4 collective-permute-done.22
  371.3 1.8 fusion.66
  (35 shorter events, 0.2 us)
Async XLA Ops:
  6.5 86.6 %all-gather.2.cloned.1.call-start = ((), (), s32[]{:S(2)}) async-start(), calls=%async_computation.1 | async-start | bytes 4456448 | tf_op jit(solution)/shard_map/all_gather | solution.py:89
  6.5 7.4 %collective-permute-start.6 = (bf16[8,128,128]{2,1,0:T(8,128)(2,1)}, bf16[8,128,128]{2,1,0:T(8,128)(2,1)S(1)}, u32[]{:S(2)}, u32[]{:S(2)}) collective-permute-start(bf16[8,128,128]{2,1,0:T(8,128)(2,1)} %bitcast.108), channel_id=1, source_target_pairs={{16,0},{32,16},{48,32},{64,48},{80,64},{96,80},{112,96},{128,112},... | collective-permute-start | bytes 786440 | tf_op jit(solution)/shard_map/ppermute | solution.py:20
  14.0 0.7 copy-start.2
  14.7 281.2 %reduce-scatter.2.cloned.1.call-start = ((), (), s32[]{:S(2)}) async-start(), calls=%async_computation.2 | async-start | bytes 3342336 | tf_op jit(solution)/shard_map/reduce_scatter | solution.py:112
  15.4 6.9 %collective-permute-start.7 = (bf16[8,2,128]{2,0,1:T(8,128)(2,1)S(1)}, bf16[8,2,128]{2,0,1:T(8,128)(2,1)S(1)}, u32[]{:S(2)}, u32[]{:S(2)}) collective-permute-start(bf16[8,2,128]{2,0,1:T(8,128)(2,1)S(1)} %bitcast.112), channel_id=1, source_target_pairs={{16,0},{32,16},{48,32},{64,48},{80,64},{96,80},{112,96},{128,112},... | collective-permute-start | bytes 12296 | tf_op jit(solution)/shard_map/ppermute | solution.py:20
  93.2 49.7 %copy-start.3 = (bf16[1,1,1,2,1024]{4,3,2,1,0:T(2,128)(2,1)S(1)}, bf16[1,1,1,2,1024]{4,3,2,1,0:T(2,128)(2,1)}, u32[]{:S(2)}) copy-start(bf16[1,1,1,2,1024]{4,3,2,1,0:T(2,128)(2,1)} %param.8) | copy-start | bytes 12292
  142.9 55.5 %copy-start.1 = (f32[1,2,128,128]{3,2,1,0:T(8,128)S(1)}, f32[1,2,128,128]{3,2,1,0:T(8,128)}, u32[]{:S(2)}) copy-start(f32[1,2,128,128]{3,2,1,0:T(8,128)} %param.12) | copy-start | bytes 393220
  142.9 153.0 %copy-start = (f32[1,128,128]{2,1,0:T(8,128)S(1)}, f32[1,128,128]{2,1,0:T(8,128)}, u32[]{:S(2)}) copy-start(f32[1,128,128]{2,1,0:T(8,128)} %param.13) | copy-start | bytes 196612
  198.5 12.8 %collective-permute-start = (f32[2,1,128]{2,1,0:T(1,128)S(1)}, f32[2,1,128]{2,1,0:T(1,128)S(1)}, u32[]{:S(2)}, u32[]{:S(2)}) collective-permute-start(f32[2,1,128]{2,1,0:T(1,128)S(1)} %get-tuple-element.20), channel_id=1, source_target_pairs={{4,0},{8,4},{12,8},{5,1},{9,5},{13,9},{6,2},{10,6},{14,10},{7,3},{... | collective-permute-start | bytes 3080 | tf_op jit(solution)/shard_map/ppermute | solution.py:31
  199.8 11.5 %collective-permute-start.1 = (f32[2,1,128]{2,1,0:T(1,128)S(1)}, f32[2,1,128]{2,1,0:T(1,128)S(1)}, u32[]{:S(2)}, u32[]{:S(2)}) collective-permute-start(f32[2,1,128]{2,1,0:T(1,128)S(1)} %get-tuple-element.19), channel_id=1, source_target_pairs={{0,4},{4,8},{8,12},{1,5},{5,9},{9,13},{2,6},{6,10},{10,14},{3,7},{... | collective-permute-start | bytes 3080 | tf_op jit(solution)/shard_map/ppermute | solution.py:30
  204.3 93.3 %collective-permute-start.4 = (f32[2,128,128]{2,1,0:T(8,128)S(1)}, f32[2,128,128]{2,1,0:T(8,128)S(1)}, u32[]{:S(2)}, u32[]{:S(2)}) collective-permute-start(f32[2,128,128]{2,1,0:T(8,128)S(1)} %bitcast.104), channel_id=1, source_target_pairs={{0,16},{16,32},{32,48},{48,64},{64,80},{80,96},{96,112},{112,128},... | collective-permute-start | bytes 393224 | tf_op jit(solution)/shard_map/ppermute | solution.py:20
  206.2 91.4 %collective-permute-start.5 = (f32[2,128,128]{2,1,0:T(8,128)S(1)}, f32[2,128,128]{2,1,0:T(8,128)S(1)}, u32[]{:S(2)}, u32[]{:S(2)}) collective-permute-start(f32[2,128,128]{2,1,0:T(8,128)S(1)} %bitcast.105), channel_id=1, source_target_pairs={{16,0},{32,16},{48,32},{64,48},{80,64},{96,80},{112,96},{128,112},... | collective-permute-start | bytes 393224 | tf_op jit(solution)/shard_map/ppermute | solution.py:20
  211.4 86.2 %collective-permute-start.2 = (f32[2,130,1]{2,1,0:T(8,128)S(1)}, f32[2,130,1]{2,1,0:T(8,128)S(1)}, u32[]{:S(2)}, u32[]{:S(2)}) collective-permute-start(f32[2,130,1]{2,1,0:T(8,128)S(1)} %get-tuple-element.11), channel_id=1, source_target_pairs={{1,0},{2,1},{3,2},{5,4},{6,5},{7,6},{9,8},{10,9},{11,10},{13,12},{... | collective-permute-start | bytes 3128 | tf_op jit(solution)/shard_map/ppermute | solution.py:31
  212.7 84.9 %collective-permute-start.3 = (f32[2,130,1]{2,1,0:T(8,128)S(1)}, f32[2,130,1]{2,1,0:T(8,128)S(1)}, u32[]{:S(2)}, u32[]{:S(2)}) collective-permute-start(f32[2,130,1]{2,1,0:T(8,128)S(1)} %get-tuple-element.12), channel_id=1, source_target_pairs={{0,1},{1,2},{2,3},{4,5},{5,6},{6,7},{8,9},{9,10},{10,11},{12,13},{... | collective-permute-start | bytes 3128 | tf_op jit(solution)/shard_map/ppermute | solution.py:30
  298.8 12.3 %collective-permute-start.8 = (f32[2,1,128]{2,1,0:T(1,128)S(1)}, f32[2,1,128]{2,1,0:T(1,128)S(1)}, u32[]{:S(2)}, u32[]{:S(2)}) collective-permute-start(f32[2,1,128]{2,1,0:T(1,128)S(1)} %get-tuple-element.18), channel_id=1, source_target_pairs={{4,0},{8,4},{12,8},{5,1},{9,5},{13,9},{6,2},{10,6},{14,10},{7,3},{... | collective-permute-start | bytes 3080 | tf_op jit(solution)/shard_map/ppermute | solution.py:31
  300.1 11.0 %collective-permute-start.9 = (f32[2,1,128]{2,1,0:T(1,128)S(1)}, f32[2,1,128]{2,1,0:T(1,128)S(1)}, u32[]{:S(2)}, u32[]{:S(2)}) collective-permute-start(f32[2,1,128]{2,1,0:T(1,128)S(1)} %get-tuple-element.17), channel_id=1, source_target_pairs={{0,4},{4,8},{8,12},{1,5},{5,9},{9,13},{2,6},{6,10},{10,14},{3,7},{... | collective-permute-start | bytes 3080 | tf_op jit(solution)/shard_map/ppermute | solution.py:30
  304.6 16.8 %collective-permute-start.12 = (f32[2,128,128]{2,1,0:T(8,128)S(1)}, f32[2,128,128]{2,1,0:T(8,128)S(1)}, u32[]{:S(2)}, u32[]{:S(2)}) collective-permute-start(f32[2,128,128]{2,1,0:T(8,128)S(1)} %fusion.63), channel_id=1, source_target_pairs={{0,16},{16,32},{32,48},{48,64},{64,80},{80,96},{96,112},{112,128},... | collective-permute-start | bytes 393224 | tf_op jit(solution)/shard_map/ppermute | solution.py:20
  306.6 14.9 %collective-permute-start.13 = (f32[2,128,128]{2,1,0:T(8,128)S(1)}, f32[2,128,128]{2,1,0:T(8,128)S(1)}, u32[]{:S(2)}, u32[]{:S(2)}) collective-permute-start(f32[2,128,128]{2,1,0:T(8,128)S(1)} %fusion.63), channel_id=1, source_target_pairs={{16,0},{32,16},{48,32},{64,48},{80,64},{96,80},{112,96},{128,112},... | collective-permute-start | bytes 393224 | tf_op jit(solution)/shard_map/ppermute | solution.py:20
  311.3 10.2 %collective-permute-start.10 = (f32[2,130,1]{2,1,0:T(8,128)S(1)}, f32[2,130,1]{2,1,0:T(8,128)S(1)}, u32[]{:S(2)}, u32[]{:S(2)}) collective-permute-start(f32[2,130,1]{2,1,0:T(8,128)S(1)} %get-tuple-element.9), channel_id=1, source_target_pairs={{1,0},{2,1},{3,2},{5,4},{6,5},{7,6},{9,8},{10,9},{11,10},{13,12},{... | collective-permute-start | bytes 3128 | tf_op jit(solution)/shard_map/ppermute | solution.py:31
  312.6 8.9 %collective-permute-start.11 = (f32[2,130,1]{2,1,0:T(8,128)S(1)}, f32[2,130,1]{2,1,0:T(8,128)S(1)}, u32[]{:S(2)}, u32[]{:S(2)}) collective-permute-start(f32[2,130,1]{2,1,0:T(8,128)S(1)} %get-tuple-element.10), channel_id=1, source_target_pairs={{0,1},{1,2},{2,3},{4,5},{5,6},{6,7},{8,9},{9,10},{10,11},{12,13},{... | collective-permute-start | bytes 3128 | tf_op jit(solution)/shard_map/ppermute | solution.py:30
  322.6 12.3 %collective-permute-start.14 = (f32[2,1,128]{2,1,0:T(1,128)S(1)}, f32[2,1,128]{2,1,0:T(1,128)S(1)}, u32[]{:S(2)}, u32[]{:S(2)}) collective-permute-start(f32[2,1,128]{2,1,0:T(1,128)S(1)} %get-tuple-element.16), channel_id=1, source_target_pairs={{4,0},{8,4},{12,8},{5,1},{9,5},{13,9},{6,2},{10,6},{14,10},{7,3},{... | collective-permute-start | bytes 3080 | tf_op jit(solution)/shard_map/ppermute | solution.py:31
  323.9 11.0 %collective-permute-start.15 = (f32[2,1,128]{2,1,0:T(1,128)S(1)}, f32[2,1,128]{2,1,0:T(1,128)S(1)}, u32[]{:S(2)}, u32[]{:S(2)}) collective-permute-start(f32[2,1,128]{2,1,0:T(1,128)S(1)} %get-tuple-element.15), channel_id=1, source_target_pairs={{0,4},{4,8},{8,12},{1,5},{5,9},{9,13},{2,6},{6,10},{10,14},{3,7},{... | collective-permute-start | bytes 3080 | tf_op jit(solution)/shard_map/ppermute | solution.py:30
  328.4 18.0 %collective-permute-start.18 = (f32[2,128,128]{2,1,0:T(8,128)S(1)}, f32[2,128,128]{2,1,0:T(8,128)S(1)}, u32[]{:S(2)}, u32[]{:S(2)}) collective-permute-start(f32[2,128,128]{2,1,0:T(8,128)S(1)} %fusion.53), channel_id=1, source_target_pairs={{0,16},{16,32},{32,48},{48,64},{64,80},{80,96},{96,112},{112,128},... | collective-permute-start | bytes 393224 | tf_op jit(solution)/shard_map/ppermute | solution.py:20
  330.3 16.1 %collective-permute-start.19 = (f32[2,128,128]{2,1,0:T(8,128)S(1)}, f32[2,128,128]{2,1,0:T(8,128)S(1)}, u32[]{:S(2)}, u32[]{:S(2)}) collective-permute-start(f32[2,128,128]{2,1,0:T(8,128)S(1)} %fusion.53), channel_id=1, source_target_pairs={{16,0},{32,16},{48,32},{64,48},{80,64},{96,80},{112,96},{128,112},... | collective-permute-start | bytes 393224 | tf_op jit(solution)/shard_map/ppermute | solution.py:20
  335.0 11.4 %collective-permute-start.16 = (f32[2,130,1]{2,1,0:T(8,128)S(1)}, f32[2,130,1]{2,1,0:T(8,128)S(1)}, u32[]{:S(2)}, u32[]{:S(2)}) collective-permute-start(f32[2,130,1]{2,1,0:T(8,128)S(1)} %get-tuple-element.7), channel_id=1, source_target_pairs={{1,0},{2,1},{3,2},{5,4},{6,5},{7,6},{9,8},{10,9},{11,10},{13,12},{... | collective-permute-start | bytes 3128 | tf_op jit(solution)/shard_map/ppermute | solution.py:31
  336.3 10.1 %collective-permute-start.17 = (f32[2,130,1]{2,1,0:T(8,128)S(1)}, f32[2,130,1]{2,1,0:T(8,128)S(1)}, u32[]{:S(2)}, u32[]{:S(2)}) collective-permute-start(f32[2,130,1]{2,1,0:T(8,128)S(1)} %get-tuple-element.8), channel_id=1, source_target_pairs={{0,1},{1,2},{2,3},{4,5},{5,6},{6,7},{8,9},{9,10},{10,11},{12,13},{... | collective-permute-start | bytes 3128 | tf_op jit(solution)/shard_map/ppermute | solution.py:30
  347.5 12.3 %collective-permute-start.20 = (f32[2,1,128]{2,1,0:T(1,128)S(1)}, f32[2,1,128]{2,1,0:T(1,128)S(1)}, u32[]{:S(2)}, u32[]{:S(2)}) collective-permute-start(f32[2,1,128]{2,1,0:T(1,128)S(1)} %get-tuple-element.14), channel_id=1, source_target_pairs={{4,0},{8,4},{12,8},{5,1},{9,5},{13,9},{6,2},{10,6},{14,10},{7,3},{... | collective-permute-start | bytes 3080 | tf_op jit(solution)/shard_map/ppermute | solution.py:31
  348.8 11.0 %collective-permute-start.21 = (f32[2,1,128]{2,1,0:T(1,128)S(1)}, f32[2,1,128]{2,1,0:T(1,128)S(1)}, u32[]{:S(2)}, u32[]{:S(2)}) collective-permute-start(f32[2,1,128]{2,1,0:T(1,128)S(1)} %get-tuple-element.13), channel_id=1, source_target_pairs={{0,4},{4,8},{8,12},{1,5},{5,9},{9,13},{2,6},{6,10},{10,14},{3,7},{... | collective-permute-start | bytes 3080 | tf_op jit(solution)/shard_map/ppermute | solution.py:30
  353.4 17.9 %collective-permute-start.24 = (f32[2,128,128]{2,1,0:T(8,128)S(1)}, f32[2,128,128]{2,1,0:T(8,128)S(1)}, u32[]{:S(2)}, u32[]{:S(2)}) collective-permute-start(f32[2,128,128]{2,1,0:T(8,128)S(1)} %fusion.43), channel_id=1, source_target_pairs={{0,16},{16,32},{32,48},{48,64},{64,80},{80,96},{96,112},{112,128},... | collective-permute-start | bytes 393224 | tf_op jit(solution)/shard_map/ppermute | solution.py:20
  355.3 16.0 %collective-permute-start.25 = (f32[2,128,128]{2,1,0:T(8,128)S(1)}, f32[2,128,128]{2,1,0:T(8,128)S(1)}, u32[]{:S(2)}, u32[]{:S(2)}) collective-permute-start(f32[2,128,128]{2,1,0:T(8,128)S(1)} %fusion.43), channel_id=1, source_target_pairs={{16,0},{32,16},{48,32},{64,48},{80,64},{96,80},{112,96},{128,112},... | collective-permute-start | bytes 393224 | tf_op jit(solution)/shard_map/ppermute | solution.py:20
  360.0 11.2 %collective-permute-start.22 = (f32[2,130,1]{2,1,0:T(8,128)S(1)}, f32[2,130,1]{2,1,0:T(8,128)S(1)}, u32[]{:S(2)}, u32[]{:S(2)}) collective-permute-start(f32[2,130,1]{2,1,0:T(8,128)S(1)} %get-tuple-element.5), channel_id=1, source_target_pairs={{1,0},{2,1},{3,2},{5,4},{6,5},{7,6},{9,8},{10,9},{11,10},{13,12},{... | collective-permute-start | bytes 3128 | tf_op jit(solution)/shard_map/ppermute | solution.py:31
  361.3 10.0 %collective-permute-start.23 = (f32[2,130,1]{2,1,0:T(8,128)S(1)}, f32[2,130,1]{2,1,0:T(8,128)S(1)}, u32[]{:S(2)}, u32[]{:S(2)}) collective-permute-start(f32[2,130,1]{2,1,0:T(8,128)S(1)} %get-tuple-element.6), channel_id=1, source_target_pairs={{0,1},{1,2},{2,3},{4,5},{5,6},{6,7},{8,9},{9,10},{10,11},{12,13},{... | collective-permute-start | bytes 3128 | tf_op jit(solution)/shard_map/ppermute | solution.py:30
Sparse Core Ops, SparseCore 0:
  14.8 78.3 all-gather.1
  198.5 97.3 reduce-scatter.1
where the time goes:
time: 385 us; the launch traced here: 380 us
  waiting for transfers between devices  113 us (29%)
  starting transfers between devices  87.6 us (23%)
  matrix products  81.9 us (21%)
  blocking collectives  49.2 us (13%)
  other arithmetic  30.8 us (8%)
  between operations  14.6 us (4%)
    reduce_scatter x1, waiting for transfers between devices, per_device(): lax.psum_scatter(row_sums(row_pick, weighted, mesh_side), ('ty', 'tx'), s...  76.1 us
    all_gather x1, blocking collectives, per_device(): piece_place = lax.all_gather(next_place, ('ty', 'tx'), axis=0, tiled=True)  49.2 us
    dot_general x1, matrix products, per_device(): jnp.einsum('ck,qk->cq', key_place, weights, precision=lax.Precision.HIGHEST)  47.5 us
    ppermute x8, starting transfers between devices, extended(): before = lax.ppermute(last, axis, up)  43.1 us
    ppermute x10, starting transfers between devices, passed_along(): return lax.ppermute(value, axis, pairs)  34.2 us
    dot_general x1, matrix products, per_device(): jnp.dot(queries, key_rows.T, preferred_element_type=jnp.float32)  26.5 us
    reduce_sum x1, other arithmetic, per_device(): row_top, denominator, summed = (new_top, jnp.sum(weights, axis=1), summed)  23.2 us
    all_gather x1, waiting for transfers between devices, per_device(): piece_keys = lax.all_gather(next_keys, ('ty', 'tx'), axis=0, tiled=True)  21.7 us
  transfers between devices with their start and end apart: 28, of which 6 were waited for; matrix products, arithmetic and copies ran while one was open for 1% of the time, Pallas kernels for 0%

commit v1 on v0

v1 whole, which is shorter than its diff:
```python
import functools
import math

import jax
import jax.numpy as jnp
from jax import lax
from jax.experimental import pallas as pl
from jax.experimental.pallas import tpu as pltpu
from jax.sharding import PartitionSpec as P

MESH = pl.DeviceIdType.MESH
BLK = 128
CAPB = 4
ITERS = 4
NEG = -1e30
SPRING_SEC = 0.5
RATE = 0.8
NT = (((1,), (1,)), ((), ()))
NN = (((1,), (0,)), ((), ()))


def remote(src, dst, send, recv, device):
    return pltpu.make_async_remote_copy(
        src_ref=src, dst_ref=dst, send_sem=send, recv_sem=recv, device_id=device, device_id_type=MESH
    )


def block_table(list_ref, count_ref, slots):
    lane = lax.broadcasted_iota(jnp.int32, (8, 128), 1)
    row = lax.broadcasted_iota(jnp.int32, (8, 128), 0)
    within = lane & 7
    wanted = jnp.zeros((8, 128), jnp.int32)
    for entry in range(slots):
        block = jnp.where(count_ref[0] > entry, list_ref[entry], -1)
        wanted = jnp.where(lane == block, 1, wanted)
    rank = jnp.zeros((8, 128), jnp.int32)
    for by in range(1, 8):
        rank = rank + jnp.where(within >= by, pltpu.roll(wanted, by, 1), 0)
    picked = jnp.where((wanted == 1) & (rank == row), within + 1, 0)
    total = picked
    for by in range(1, 8):
        total = total + pltpu.roll(picked, 128 - by, 1)
    return jnp.where(total == 0, 8, total - 1)


def kernel(
    sizes, list_ref, count_ref, desc, pos, ids, disp, stiff, out,
    qbuf, kin0, kin1, kin2, kin3, pin, kwork, vwork, tabv, tabs, idb, onea, onec, mcount,
    acc, mx, part, prt, pull, pbuf, scat, ub, lob, upb, edge, halo,
    qs, qr, hs, hr, ks, kr, ts, tr, tl, ids_s, ids_r, ps, pr, cs, cr, us, ur,
):
    ns, ny, nz, slots = sizes
    plane = ny * nz
    pts, feat = desc.shape
    half = pts // 2
    blocks = pts // BLK
    side = stiff.shape[0]
    s, y, z = lax.axis_index("sec"), lax.axis_index("ty"), lax.axis_index("tx")
    me = y * nz + z
    right, left = {"tx": lax.rem(z + 1, nz)}, {"tx": lax.rem(z + nz - 1, nz)}
    across = {"tx": lax.rem(z + 2, nz)}
    down, up = {"ty": lax.rem(y + 1, ny)}, {"ty": lax.rem(y + ny - 1, ny)}
    after, before = {"sec": lax.rem(s + 1, ns)}, {"sec": lax.rem(s + ns - 1, ns)}

    def peer(by):
        tile = lax.rem(me + by, plane)
        return tile, {"ty": lax.div(tile, nz), "tx": lax.rem(tile, nz)}

    barrier = pltpu.get_barrier_semaphore()

    def greet(by, carry):
        pl.semaphore_signal(barrier, inc=1, device_id=peer(by)[1], device_id_type=MESH)
        return carry

    lax.fori_loop(1, plane, greet, 0)
    for device in (after, before):
        pl.semaphore_signal(barrier, inc=1, device_id=device, device_id_type=MESH)

    tabv[0] = block_table(list_ref, count_ref, slots)
    qbuf[0] = desc[...]
    idb[pl.ds(me, 1)] = ids[...][None]
    acc[...] = jnp.zeros_like(acc)
    mx[...] = jnp.full_like(mx, NEG)
    mcount[...] = jnp.zeros_like(mcount)
    scat[...] = jnp.zeros_like(scat)

    pl.semaphore_wait(barrier, plane + 1)

    rows = [pl.ds(0, half), pl.ds(half, half)]
    shift = [
        remote(desc.at[rows[0]], kin0.at[rows[0]], hs.at[0], hr.at[0], before),
        remote(desc.at[rows[1]], kin0.at[rows[1]], hs.at[1], hr.at[1], before),
        remote(pos, pin.at[0], hs.at[2], hr.at[2], before),
    ]
    tables = [
        remote(tabv.at[0], tabv.at[1], ts.at[0], tr.at[0], right),
        remote(tabv.at[0], tabv.at[2], ts.at[1], tr.at[1], left),
        remote(tabv.at[0], tabv.at[3], ts.at[2], tr.at[2], across),
    ]
    queries = [
        remote(desc.at[rows[0]], qbuf.at[1, rows[0]], qs.at[0], qr.at[0], right),
        remote(desc.at[rows[1]], qbuf.at[2, rows[1]], qs.at[1], qr.at[1], left),
        remote(desc.at[rows[1]], qbuf.at[1, rows[1]], qs.at[2], qr.at[2], right),
        remote(desc.at[rows[0]], qbuf.at[2, rows[0]], qs.at[3], qr.at[3], left),
        remote(qbuf.at[1, rows[0]], qbuf.at[3, rows[0]], qs.at[4], qr.at[4], right),
        remote(qbuf.at[2, rows[1]], qbuf.at[3, rows[1]], qs.at[5], qr.at[5], left),
    ]
    keys = [
        remote(kin0.at[rows[0]], kin1.at[rows[0]], ks.at[0], kr.at[0], down),
        remote(kin0.at[rows[1]], kin2.at[rows[1]], ks.at[1], kr.at[1], up),
        remote(kin0.at[rows[1]], kin1.at[rows[1]], ks.at[2], kr.at[2], down),
        remote(kin0.at[rows[0]], kin2.at[rows[0]], ks.at[3], kr.at[3], up),
        remote(kin1.at[rows[0]], kin3.at[rows[0]], ks.at[4], kr.at[4], down),
        remote(kin2.at[rows[1]], kin3.at[rows[1]], ks.at[5], kr.at[5], up),
        remote(pin.at[0], pin.at[1], ks.at[6], kr.at[6], down),
        remote(pin.at[0], pin.at[2], ks.at[7], kr.at[7], up),
        remote(pin.at[1], pin.at[3], ks.at[8], kr.at[8], down),
    ]
    partials = [
        remote(part.at[1], prt.at[2], cs.at[0], cr.at[0], left),
        remote(part.at[2], prt.at[1], cs.at[1], cr.at[1], right),
        remote(part.at[3], prt.at[3], cs.at[2], cr.at[2], across),
    ]

    def exchange(turn):
        source = disp if turn == 0 else ub.at[turn - 1]
        return [
            remote(edge.at[turn, 0], halo.at[turn, 1], us.at[turn, 0], ur.at[turn, 0], up),
            remote(edge.at[turn, 1], halo.at[turn, 0], us.at[turn, 1], ur.at[turn, 1], down),
            remote(edge.at[turn, 2], halo.at[turn, 3], us.at[turn, 2], ur.at[turn, 2], left),
            remote(edge.at[turn, 3], halo.at[turn, 2], us.at[turn, 3], ur.at[turn, 3], right),
            remote(source, lob.at[turn], us.at[turn, 4], ur.at[turn, 4], after),
            remote(source, upb.at[turn], us.at[turn, 5], ur.at[turn, 5], before),
        ]

    swaps = [exchange(turn) for turn in range(ITERS)]

    def ids_copy(by):
        _, device = peer(by)
        return remote(idb.at[me], idb.at[me], ids_s.at[by], ids_r.at[me], device)

    def ids_from(tile):
        return remote(idb.at[tile], idb.at[tile], ids_s.at[0], ids_r.at[tile], before)

    def pull_copy(by):
        _, device = peer(by)
        return remote(pull, pbuf.at[me], ps.at[by], pr.at[me], device)

    def pull_from(tile):
        return remote(pull, pbuf.at[tile], ps.at[0], pr.at[tile], before)

    def start_ids(by, carry):
        ids_copy(by).start()
        return carry

    for copy in shift[:2]:
        copy.start()
    for copy in tables:
        copy.start()
    for copy in queries[:4]:
        copy.start()
    shift[2].start()
    lax.fori_loop(1, plane, start_ids, 0)

    def set_key(slot, source):
        kwork[slot] = source[...].reshape(blocks, BLK, feat)
        place = pin[slot].astype(jnp.float32)
        line = lax.broadcasted_iota(jnp.int32, (16, pts), 0)
        value = jnp.where(line == 2, 1.0, 0.0)
        value = jnp.where(line == 1, place[1:2], value)
        value = jnp.where(line == 0, place[0:1], value).astype(jnp.bfloat16)
        for block in range(blocks):
            vwork[slot, block] = value[:, block * BLK : (block + 1) * BLK]

    eye = lax.broadcasted_iota(jnp.int32, (side, side), 0) == lax.broadcasted_iota(jnp.int32, (side, side), 1)

    def set_edges(turn, channel, value):
        edge[turn, 0, channel : channel + 1, :] = value[0:1, :]
        edge[turn, 1, channel : channel + 1, :] = value[side - 1 : side, :]
        for at, column in ((2, value[:, 0:1]), (3, value[:, side - 1 : side])):
            spread = jnp.where(eye, jnp.broadcast_to(column, (side, side)), 0.0)
            edge[turn, at, channel : channel + 1, :] = jnp.sum(spread, axis=0, keepdims=True)

    for channel in range(2):
        set_edges(0, channel, disp[channel])

    def one_hots(by, carry):
        tile, _ = peer(by)

        @pl.when(by > 0)
        def _():
            ids_from(tile).wait_recv()

        vertex = idb[tile]
        level = lax.broadcasted_iota(jnp.int32, (side, pts), 0)
        pick_row = level == ((vertex - me * (side * side)) >> 7)
        pick_col = level == (vertex & (side - 1))
        row_hot = jnp.where(pick_row, 1.0, 0.0).astype(jnp.bfloat16)
        col_hot = jnp.where(pick_col, 1.0, 0.0).astype(jnp.bfloat16)
        onea[tile] = row_hot
        onec[tile] = col_hot
        mcount[...] += lax.dot_general(row_hot, col_hot, NT, preferred_element_type=jnp.float32)
        return carry

    factor = 16.0 / feat * math.log2(math.e)
    chunk = 256

    def match(step, carry):
        q, k = lax.div(step, 4), lax.rem(step, 4)

        @pl.when(step == 1)
        def _():
            queries[0].wait_recv()
            queries[4].start()
            queries[1].wait_recv()
            queries[5].start()
            keys[0].wait_recv()
            keys[4].start()
            keys[1].wait_recv()
            keys[5].start()
            keys[6].wait_recv()
            keys[8].start()
            lax.fori_loop(0, plane, one_hots, 0)
            keys[2].wait_recv()
            set_key(1, kin1)

        @pl.when(step == 2)
        def _():
            keys[3].wait_recv()
            keys[7].wait_recv()
            set_key(2, kin2)

        @pl.when(step == 3)
        def _():
            keys[4].wait_recv()
            keys[5].wait_recv()
            keys[8].wait_recv()
            set_key(3, kin3)

        for slot in range(1, 4):

            @pl.when(step == 4 * slot)
            def _():
                for copy in ((), (2,), (3,), (4, 5))[slot]:
                    queries[copy].wait_recv()
                tables[slot - 1].wait_recv()
                local = pltpu.make_async_copy(tabv.at[slot], tabs.at[slot], tl.at[slot])
                local.start()
                local.wait()

        @pl.when(step == 12)
        def _():
            for copy in swaps[0]:
                copy.start()

        key_row = lax.rem(y + jnp.where(k == 1, ny - 1, jnp.where(k == 2, 1, jnp.where(k == 3, 2, 0))), ny)
        lane = (key_row * nz + z) * 8
        codes = [tabs[q, slot, lane] for slot in range(CAPB)]
        found = [code & (blocks - 1) for code in codes]
        biases = [jnp.where(code < blocks, 0.0, NEG) for code in codes]
        key_rows = jnp.concatenate([kwork[k, block] for block in found], axis=0)
        values = jnp.concatenate([vwork[k, block] for block in found], axis=1)
        for at in range(pts // chunk):
            cols = pl.ds(at * chunk, chunk)
            scores = lax.dot_general(key_rows, qbuf[q, cols, :], NT, preferred_element_type=jnp.float32)
            scores = jnp.concatenate(
                [scores[i * BLK : (i + 1) * BLK] * factor + biases[i] for i in range(CAPB)], axis=0
            )
            old = mx[q, :, cols]
            new = jnp.maximum(old, jnp.max(scores, axis=0, keepdims=True))
            weights = jnp.exp2(scores - new).astype(jnp.bfloat16)
            added = lax.dot_general(values, weights, NN, preferred_element_type=jnp.float32)
            acc[q, :, cols] = acc[q, :, cols] * jnp.exp2(old - new) + added
            mx[q, :, cols] = new

        @pl.when(k == 3)
        def _():
            part[q, 0:3, :] = acc[q, 0:3, :]
            part[q, 3:4, :] = mx[q]

        for slot in range(1, 4):

            @pl.when(step == 4 * slot + 3)
            def _():
                partials[slot - 1].start()

        return carry

    local = pltpu.make_async_copy(tabv.at[0], tabs.at[0], tl.at[0])
    local.start()
    local.wait()
    shift[0].wait_recv()
    keys[0].start()
    shift[1].wait_recv()
    keys[1].start()
    keys[2].start()
    keys[3].start()
    shift[2].wait_recv()
    keys[6].start()
    keys[7].start()
    set_key(0, kin0)
    lax.fori_loop(0, 16, match, 0)

    has_next = s < ns - 1
    for copy in partials:
        copy.wait_recv()
    pieces = [part[0]] + [prt[slot] for slot in range(1, 4)]
    top = functools.reduce(jnp.maximum, [piece[3:4] for piece in pieces])
    scaled = [piece[0:3] * jnp.exp2(piece[3:4] - top) for piece in pieces]
    total = functools.reduce(jnp.add, scaled)
    mine = pos[...].astype(jnp.float32)
    pull[...] = jnp.where(has_next, total[0:2] / total[2:3] - mine, 0.0)

    def start_pull(by, carry):
        pull_copy(by).start()
        return carry

    lax.fori_loop(1, plane, start_pull, 0)
    pbuf[pl.ds(me, 1)] = pull[...][None]

    def gather_pull(by, carry):
        tile, _ = peer(by)

        @pl.when(by > 0)
        def _():
            pull_from(tile).wait_recv()

        row_hot = onea[tile].reshape(side // 16, 16, pts)
        pieces = []
        for channel in range(2):
            value = jnp.broadcast_to(pbuf[tile, channel : channel + 1, :], (16, pts))
            high = value.astype(jnp.bfloat16)
            low = (value - high.astype(jnp.float32)).astype(jnp.bfloat16)
            for piece in (high, low):
                pieces.append((row_hot * piece[None]).reshape(side, pts))
        stacked = jnp.concatenate(pieces, axis=0)
        scat[...] += lax.dot_general(stacked, onec[tile], NT, preferred_element_type=jnp.float32)
        return carry

    lax.fori_loop(0, plane, gather_pull, 0)

    flag = lambda test: jnp.where(test, 1.0, 0.0)
    next_flag, last_flag = flag(s < ns - 1), flag(s > 0)
    linked = next_flag + last_flag
    matched = mcount[...] * next_flag
    gains = stiff[...]
    inverse = RATE / (4.0 * gains + SPRING_SEC * linked + matched)
    pulled = [scat[0:side] + scat[side : 2 * side], scat[2 * side : 3 * side] + scat[3 * side :]]
    row_at = lax.broadcasted_iota(jnp.int32, (side, side), 0)
    col_at = lax.broadcasted_iota(jnp.int32, (side, side), 1)
    flags = [flag(y > 0), flag(y < ny - 1), flag(z > 0), flag(z < nz - 1)]

    for turn in range(ITERS):
        for copy in swaps[turn]:
            copy.wait_recv()
        for channel in range(2):
            value = disp[channel] if turn == 0 else ub[turn - 1, channel]
            lines = [halo[turn, at, channel : channel + 1, :] * flags[at] for at in range(4)]
            cols = [
                jnp.sum(jnp.where(eye, jnp.broadcast_to(line, (side, side)), 0.0), axis=1, keepdims=True)
                for line in lines[2:]
            ]
            around = jnp.where(row_at == 0, lines[0], pltpu.roll(value, 1, 0))
            around += jnp.where(row_at == side - 1, lines[1], pltpu.roll(value, side - 1, 0))
            around += jnp.where(col_at == 0, cols[0], pltpu.roll(value, 1, 1))
            around += jnp.where(col_at == side - 1, cols[1], pltpu.roll(value, side - 1, 1))
            force = gains * (around - 4.0 * value) + pulled[channel] - matched * value
            force += SPRING_SEC * (
                lob[turn, channel] * last_flag + upb[turn, channel] * next_flag - linked * value
            )
            moved = value + force * inverse
            if turn == ITERS - 1:
                out[channel] = moved
            else:
                ub[turn, channel] = moved
                set_edges(turn + 1, channel, moved)
        if turn < ITERS - 1:
            for copy in swaps[turn + 1]:
                copy.start()

    for copy in shift + tables + queries + keys + partials + [c for swap in swaps for c in swap]:
        copy.wait_send()

    def finish(by, carry):
        ids_copy(by).wait_send()
        pull_copy(by).wait_send()
        return carry

    lax.fori_loop(1, plane, finish, 0)


def solution(mesh):
    ns, ny, nz = mesh.shape["sec"], mesh.shape["ty"], mesh.shape["tx"]

    def per_device(desc, pos, ids, blocks, count, disp, stiff):
        desc, pos, ids = desc[0, 0, 0], pos[0, 0, 0], ids[0, 0]
        blocks, count = blocks[0, 0, 0], count.reshape(1)
        disp, stiff = disp[0], stiff[0]
        pts, feat = desc.shape
        side = stiff.shape[0]
        plane = ny * nz
        bf16, f32, i32 = jnp.bfloat16, jnp.float32, jnp.int32
        tile = pltpu.VMEM((pts, feat), bf16)
        dma = pltpu.SemaphoreType.DMA
        smem = pl.BlockSpec(memory_space=pltpu.SMEM)
        vmem = pl.BlockSpec(memory_space=pltpu.VMEM)
        moved = pl.pallas_call(
            functools.partial(kernel, (ns, ny, nz, blocks.shape[0])),
            out_shape=jax.ShapeDtypeStruct(disp.shape, f32),
            in_specs=[smem, smem] + [vmem] * 5,
            out_specs=vmem,
            scratch_shapes=[
                pltpu.VMEM((4, pts, feat), bf16),
                tile, tile, tile, tile,
                pltpu.VMEM((4, 2, pts), bf16),
                pltpu.VMEM((4, pts // BLK, BLK, feat), bf16),
                pltpu.VMEM((4, pts // BLK, 16, BLK), bf16),
                pltpu.VMEM((4, 8, 128), i32),
                pltpu.SMEM((4, 8, 128), i32),
                pltpu.VMEM((plane, 1, pts), i32),
                pltpu.VMEM((plane, side, pts), bf16),
                pltpu.VMEM((plane, side, pts), bf16),
                pltpu.VMEM((side, side), f32),
                pltpu.VMEM((4, 16, pts), f32),
                pltpu.VMEM((4, 1, pts), f32),
                pltpu.VMEM((4, 4, pts), f32),
                pltpu.VMEM((4, 4, pts), f32),
                pltpu.VMEM((2, pts), f32),
                pltpu.VMEM((plane, 2, pts), f32),
                pltpu.VMEM((4 * side, side), f32),
                pltpu.VMEM((ITERS - 1, 2, side, side), f32),
                pltpu.VMEM((ITERS, 2, side, side), f32),
                pltpu.VMEM((ITERS, 2, side, side), f32),
                pltpu.VMEM((ITERS, 4, 2, side), f32),
                pltpu.VMEM((ITERS, 4, 2, side), f32),
                dma((6,)), dma((6,)),
                dma((3,)), dma((3,)),
                dma((9,)), dma((9,)),
                dma((3,)), dma((3,)), dma((4,)),
                dma((plane,)), dma((plane,)),
                dma((plane,)), dma((plane,)),
                dma((3,)), dma((3,)),
                dma((ITERS, 6)), dma((ITERS, 6)),
            ],
            compiler_params=pltpu.CompilerParams(
                collective_id=0, has_side_effects=True, vmem_limit_bytes=56 * 1024 * 1024
            ),
        )(blocks, count, desc, pos, ids, disp, stiff)
        return moved[None]

    in_specs = (
        P("sec", "ty", "tx", None, None),
        P("sec", "ty", "tx", None, None),
        P("sec", "ty", "tx", None),
        P("sec", "ty", "tx", None),
        P("sec", "ty", "tx"),
        P("sec", None, "ty", "tx"),
        P("sec", "ty", "tx"),
    )
    return jax.shard_map(
        per_device, mesh=mesh, in_specs=in_specs, out_specs=P("sec", None, "ty", "tx"), check_vma=False
    )
```

time: 385 us -> 99.4 us (0.26); the launches traced: 380 us -> 98.9 us
  waiting for transfers between devices: 113 us -> 0 us
  Pallas kernels: 0 us -> 96.7 us
  starting transfers between devices: 87.6 us -> 0 us
  matrix products: 81.9 us -> 0 us
  blocking collectives: 49.2 us -> 0 us
  other arithmetic: 30.8 us -> 0 us
  between operations: 14.6 us -> 0.66 us
    pallas_call x0 -> x1, Pallas kernels: none -> 96.7 us  [per_device(): pl.pallas_call(functools.partial(kernel, (ns, ny, nz, blocks.shape[0])),...]
    ppermute x26 -> x0, starting transfers between devices: 87.6 us -> none  [the longest x8 43.1 us: extended(): before = lax.ppermute(last, axis, up)]
    dot_general x3 -> x0, matrix products: 81.9 us -> none  [the longest x1 47.5 us: per_device(): jnp.einsum('ck,qk->cq', key_place, weights, precision=lax.Precision.HIGHEST)]
    reduce_scatter x1 -> x0, waiting for transfers between devices: 76.1 us -> none  [per_device(): lax.psum_scatter(row_sums(row_pick, weighted, mesh_side), ('ty', 'tx'), s...]
    all_gather x1 -> x0, blocking collectives: 49.2 us -> none  [per_device(): piece_place = lax.all_gather(next_place, ('ty', 'tx'), axis=0, tiled=True)]
    reduce_sum x1 -> x0, other arithmetic: 23.2 us -> none  [per_device(): row_top, denominator, summed = (new_top, jnp.sum(weights, axis=1), summed)]
    all_gather x1 -> x0, waiting for transfers between devices: 21.7 us -> none  [per_device(): piece_keys = lax.all_gather(next_keys, ('ty', 'tx'), axis=0, tiled=True)]
    ppermute x26 -> x0, waiting for transfers between devices: 15.3 us -> none  [the longest x8 11.1 us: extended(): after = lax.ppermute(initial, axis, down)]
  transfers between devices with their start and end apart: 28 -> 0, of which waited for: 6 -> 0; matrix products, arithmetic and copies ran while one was open for 1% -> 0% of each run, Pallas kernels for 0% -> 0%
where the time goes in v1:
time: 99.4 us; the launch traced here: 98.9 us
  Pallas kernels  96.7 us (97%)
  local copies, waits for them, and re-layouts  1.57 us (2%)
    pallas_call x1, Pallas kernels, per_device(): pl.pallas_call(functools.partial(kernel, (ns, ny, nz, blocks.shape[0])),...  96.7 us

profile of v1, /device:TPU:4, one launch (start us, length us, event | category | flops | bytes accessed | tf_op | source)
XLA Modules:
  0.0 98.9 jit_solution(10515729064656205588)
XLA Ops:
  0.7 96.7 %shard_map.73 = f32[2,128,128]{2,1,0:T(8,128)} custom-call(s32[32]{0:T(128)} %bitcast.15, s32[1]{0:T(128)} %bitcast.8.count_ref, bf16[1024,128]{1,0:T(8,128)(2,1)} %bitcast.10, bf16[2,1024]{1,0:T(2,128)(2,1)} %bitcast.13, s32[1,1024]{1,0:T(1,128)} %bitcast.14, f32[2,128,128]{2,1,0:T(8,128)} %bitcast.11, f32[128,128]{1,0:T(8,128)} %bitcast.12), custom_call_target="tpu_custom_call" | custom-call | tf_op jit(solution)/shard_map/pallas_call | solution.py:407
  97.4 1.6 %copy.10 = f32[1,2,128,128]{3,2,1,0:T(8,128)} copy(f32[1,2,128,128]{3,2,1,0:T(8,128)} %bitcast.9) | data formatting | bytes 262144

commit v2 on v1

--- a/solution.py
+++ b/solution.py
@@ -11,6 +11,7 @@
 MESH = pl.DeviceIdType.MESH
 BLK = 128
 CAPB = 4
+CHUNK = 256
 ITERS = 4
 NEG = -1e30
 SPRING_SEC = 0.5
@@ -31,7 +32,7 @@
     within = lane & 7
     wanted = jnp.zeros((8, 128), jnp.int32)
     for entry in range(slots):
-        block = jnp.where(count_ref[0] > entry, list_ref[entry], -1)
+        block = jnp.where(count_ref[0, 0, 0] > entry, list_ref[entry], -1)
         wanted = jnp.where(lane == block, 1, wanted)
     rank = jnp.zeros((8, 128), jnp.int32)
     for by in range(1, 8):
@@ -45,9 +46,9 @@
 
 def kernel(
     sizes, list_ref, count_ref, desc, pos, ids, disp, stiff, out,
-    qbuf, kin0, kin1, kin2, kin3, pin, kwork, vwork, tabv, tabs, idb, onea, onec, mcount,
-    acc, mx, part, prt, pull, pbuf, scat, ub, lob, upb, edge, halo,
-    qs, qr, hs, hr, ks, kr, ts, tr, tl, ids_s, ids_r, ps, pr, cs, cr, us, ur,
+    dispv, stiffv, posv, qbuf, kin0, kin1, kin2, kin3, pin, kwork, vwork, tabv, tabs, idb, onea, onec, mcount,
+    acc, mx, sbuf0, sbuf1, tops0, tops1, part, prt, pull, pbuf, scat, ub, wire, lob, upb, edge, halo,
+    qs, qr, hs, hr, ks, kr, ts, tr, tl, ids_s, ids_r, ps, pr, cs, cr, us, ur, ls, gossip,
 ):
     ns, ny, nz, slots = sizes
     plane = ny * nz
@@ -68,23 +69,26 @@
 
     barrier = pltpu.get_barrier_semaphore()
 
-    def greet(by, carry):
-        pl.semaphore_signal(barrier, inc=1, device_id=peer(by)[1], device_id_type=MESH)
-        return carry
-
-    lax.fori_loop(1, plane, greet, 0)
-    for device in (after, before):
+    near = (right, left, down, up, after, before)
+    for device in near:
         pl.semaphore_signal(barrier, inc=1, device_id=device, device_id_type=MESH)
+    loads = [
+        pltpu.make_async_copy(desc, qbuf.at[0], ls.at[0]),
+        pltpu.make_async_copy(pos, posv, ls.at[1]),
+        pltpu.make_async_copy(ids, idb.at[me], ls.at[2]),
+        pltpu.make_async_copy(disp, dispv, ls.at[3]),
+        pltpu.make_async_copy(stiff, stiffv, ls.at[4]),
+    ]
+    for copy in loads:
+        copy.start()
 
     tabv[0] = block_table(list_ref, count_ref, slots)
-    qbuf[0] = desc[...]
-    idb[pl.ds(me, 1)] = ids[...][None]
     acc[...] = jnp.zeros_like(acc)
     mx[...] = jnp.full_like(mx, NEG)
     mcount[...] = jnp.zeros_like(mcount)
     scat[...] = jnp.zeros_like(scat)
 
-    pl.semaphore_wait(barrier, plane + 1)
+    pl.semaphore_wait(barrier, len(near))
 
     rows = [pl.ds(0, half), pl.ds(half, half)]
     shift = [
@@ -123,24 +127,25 @@
     ]
 
     def exchange(turn):
-        source = disp if turn == 0 else ub.at[turn - 1]
         return [
             remote(edge.at[turn, 0], halo.at[turn, 1], us.at[turn, 0], ur.at[turn, 0], up),
             remote(edge.at[turn, 1], halo.at[turn, 0], us.at[turn, 1], ur.at[turn, 1], down),
             remote(edge.at[turn, 2], halo.at[turn, 3], us.at[turn, 2], ur.at[turn, 2], left),
             remote(edge.at[turn, 3], halo.at[turn, 2], us.at[turn, 3], ur.at[turn, 3], right),
-            remote(source, lob.at[turn], us.at[turn, 4], ur.at[turn, 4], after),
-            remote(source, upb.at[turn], us.at[turn, 5], ur.at[turn, 5], before),
+            remote(wire.at[turn, 0], lob.at[turn, 0], us.at[turn, 4], ur.at[turn, 4], after),
+            remote(wire.at[turn, 0], upb.at[turn, 0], us.at[turn, 5], ur.at[turn, 5], before),
+            remote(wire.at[turn, 1], lob.at[turn, 1], us.at[turn, 6], ur.at[turn, 6], after),
+            remote(wire.at[turn, 1], upb.at[turn, 1], us.at[turn, 7], ur.at[turn, 7], before),
         ]
 
     swaps = [exchange(turn) for turn in range(ITERS)]
 
     def ids_copy(by):
         _, device = peer(by)
-        return remote(idb.at[me], idb.at[me], ids_s.at[by], ids_r.at[me], device)
+        return remote(ids, idb.at[me], ids_s.at[by], ids_r.at[me], device)
 
     def ids_from(tile):
-        return remote(idb.at[tile], idb.at[tile], ids_s.at[0], ids_r.at[tile], before)
+        return remote(ids, idb.at[tile], ids_s.at[0], ids_r.at[tile], before)
 
     def pull_copy(by):
         _, device = peer(by)
@@ -153,14 +158,18 @@
         ids_copy(by).start()
         return carry
 
-    for copy in shift[:2]:
+    for copy in shift[:2] + tables[:2] + queries[:2] + shift[2:]:
         copy.start()
-    for copy in tables:
+    for at, pair in enumerate(((right, left), (down, up), (down, up))):
+        for device in pair:
+            pl.semaphore_signal(gossip.at[at], inc=1, device_id=device, device_id_type=MESH)
+        pl.semaphore_wait(gossip.at[at], 2)
+    lax.fori_loop(1, plane, start_ids, 0)
+    tables[2].start()
+    for copy in queries[2:4]:
         copy.start()
-    for copy in queries[:4]:
-        copy.start()
-    shift[2].start()
-    lax.fori_loop(1, plane, start_ids, 0)
+    for copy in loads:
+        copy.wait()
 
     def set_key(slot, source):
         kwork[slot] = source[...].reshape(blocks, BLK, feat)
@@ -182,7 +191,8 @@
             edge[turn, at, channel : channel + 1, :] = jnp.sum(spread, axis=0, keepdims=True)
 
     for channel in range(2):
-        set_edges(0, channel, disp[channel])
+        set_edges(0, channel, dispv[channel])
+        wire[0, channel] = dispv[channel].astype(jnp.bfloat16)
 
     def one_hots(by, carry):
         tile, _ = peer(by)
@@ -203,12 +213,51 @@
         return carry
 
     factor = 16.0 / feat * math.log2(math.e)
-    chunk = 256
+
+    def found(step):
+        q, k = lax.div(step, 4), lax.rem(step, 4)
+        key_row = lax.rem(y + jnp.where(k == 1, ny - 1, jnp.where(k == 2, 1, jnp.where(k == 3, 2, 0))), ny)
+        lane = (key_row * nz + z) * 8
+        codes = [tabs[q, slot, lane] for slot in range(CAPB)]
+        return q, k, [code & (blocks - 1) for code in codes], [code < blocks for code in codes]
+
+    chunks = [pl.ds(at * CHUNK, CHUNK) for at in range(pts // CHUNK)]
+
+    def scorer(step, sbuf, tops):
+        q, k, at_block, live = found(step)
+        key_rows = jnp.concatenate([kwork[k, block] for block in at_block], axis=0)
+
+        def score(cols):
+            raw = lax.dot_general(key_rows, qbuf[q, cols, :], NT, preferred_element_type=jnp.float32)
+            sbuf[:, cols] = raw
+            for i in range(CAPB):
+                top = jnp.max(raw[i * BLK : (i + 1) * BLK], axis=0, keepdims=True)
+                tops[i, :, cols] = jnp.where(live[i], top, NEG)
+
+        return score
+
+    def weigher(step, sbuf, tops):
+        q, k, at_block, live = found(step)
+        values = jnp.concatenate([vwork[k, block] for block in at_block], axis=1)
+
+        def weigh(cols):
+            old = mx[q, :, cols]
+            new = functools.reduce(jnp.maximum, [tops[i, :, cols] for i in range(CAPB)], old)
+            weights = []
+            for i in range(CAPB):
+                base = jnp.where(live[i], new, -NEG)
+                raw = sbuf[i * BLK : (i + 1) * BLK, cols]
+                weights.append(jnp.exp2((raw - base) * factor).astype(jnp.bfloat16))
+            added = lax.dot_general(
+                values, jnp.concatenate(weights, axis=0), NN, preferred_element_type=jnp.float32
+            )
+            acc[q, :, cols] = acc[q, :, cols] * jnp.exp2((old - new) * factor) + added
+            mx[q, :, cols] = new
+
+        return weigh
 
     def match(step, carry):
-        q, k = lax.div(step, 4), lax.rem(step, 4)
-
-        @pl.when(step == 1)
+        @pl.when(step == 0)
         def _():
             queries[0].wait_recv()
             queries[4].start()
@@ -224,13 +273,13 @@
             keys[2].wait_recv()
             set_key(1, kin1)
 
-        @pl.when(step == 2)
+        @pl.when(step == 1)
         def _():
             keys[3].wait_recv()
             keys[7].wait_recv()
             set_key(2, kin2)
 
-        @pl.when(step == 3)
+        @pl.when(step == 2)
         def _():
             keys[4].wait_recv()
             keys[5].wait_recv()
@@ -239,7 +288,7 @@
 
         for slot in range(1, 4):
 
-            @pl.when(step == 4 * slot)
+            @pl.when(step == 4 * slot - 1)
             def _():
                 for copy in ((), (2,), (3,), (4, 5))[slot]:
                     queries[copy].wait_recv()
@@ -248,30 +297,22 @@
                 local.start()
                 local.wait()
 
-        @pl.when(step == 12)
+        @pl.when(step == 10)
         def _():
             for copy in swaps[0]:
                 copy.start()
 
-        key_row = lax.rem(y + jnp.where(k == 1, ny - 1, jnp.where(k == 2, 1, jnp.where(k == 3, 2, 0))), ny)
-        lane = (key_row * nz + z) * 8
-        codes = [tabs[q, slot, lane] for slot in range(CAPB)]
-        found = [code & (blocks - 1) for code in codes]
-        biases = [jnp.where(code < blocks, 0.0, NEG) for code in codes]
-        key_rows = jnp.concatenate([kwork[k, block] for block in found], axis=0)
-        values = jnp.concatenate([vwork[k, block] for block in found], axis=1)
-        for at in range(pts // chunk):
-            cols = pl.ds(at * chunk, chunk)
-            scores = lax.dot_general(key_rows, qbuf[q, cols, :], NT, preferred_element_type=jnp.float32)
-            scores = jnp.concatenate(
-                [scores[i * BLK : (i + 1) * BLK] * factor + biases[i] for i in range(CAPB)], axis=0
-            )
-            old = mx[q, :, cols]
-            new = jnp.maximum(old, jnp.max(scores, axis=0, keepdims=True))
-            weights = jnp.exp2(scores - new).astype(jnp.bfloat16)
-            added = lax.dot_general(values, weights, NN, preferred_element_type=jnp.float32)
-            acc[q, :, cols] = acc[q, :, cols] * jnp.exp2(old - new) + added
-            mx[q, :, cols] = new
+        following = lax.rem(step + 1, 16)
+        for parity, first, second in ((0, (sbuf0, tops0), (sbuf1, tops1)), (1, (sbuf1, tops1), (sbuf0, tops0))):
+
+            @pl.when(lax.rem(step, 2) == parity)
+            def _():
+                score, weigh = scorer(following, *second), weigher(step, *first)
+                for cols in chunks:
+                    weigh(cols)
+                    score(cols)
+
+        q, k = lax.div(step, 4), lax.rem(step, 4)
 
         @pl.when(k == 3)
         def _():
@@ -299,6 +340,9 @@
     keys[6].start()
     keys[7].start()
     set_key(0, kin0)
+    score = scorer(jnp.int32(0), sbuf0, tops0)
+    for cols in chunks:
+        score(cols)
     lax.fori_loop(0, 16, match, 0)
 
     has_next = s < ns - 1
@@ -306,9 +350,9 @@
         copy.wait_recv()
     pieces = [part[0]] + [prt[slot] for slot in range(1, 4)]
     top = functools.reduce(jnp.maximum, [piece[3:4] for piece in pieces])
-    scaled = [piece[0:3] * jnp.exp2(piece[3:4] - top) for piece in pieces]
+    scaled = [piece[0:3] * jnp.exp2((piece[3:4] - top) * factor) for piece in pieces]
     total = functools.reduce(jnp.add, scaled)
-    mine = pos[...].astype(jnp.float32)
+    mine = posv[...].astype(jnp.float32)
     pull[...] = jnp.where(has_next, total[0:2] / total[2:3] - mine, 0.0)
 
     def start_pull(by, carry):
@@ -318,10 +362,18 @@
     lax.fori_loop(1, plane, start_pull, 0)
     pbuf[pl.ds(me, 1)] = pull[...][None]
 
-    def gather_pull(by, carry):
-        tile, _ = peer(by)
-
-        @pl.when(by > 0)
+    order = [(0, 0), (1, 0), (3, 0), (2, 0), (0, 1), (0, 3), (1, 1), (3, 1), (1, 3), (3, 3)]
+    order += [(2, 1), (2, 3), (0, 2), (1, 2), (3, 2), (2, 2)]
+    wrap = lambda value: value - (1 << 32) if value >= 1 << 31 else value
+    code_y = wrap(sum(dy << (2 * at) for at, (dy, _) in enumerate(order)))
+    code_z = wrap(sum(dz << (2 * at) for at, (_, dz) in enumerate(order)))
+
+    def gather_pull(turn, carry):
+        ahead_y = (jnp.int32(code_y) >> (2 * turn)) & 3
+        ahead_z = (jnp.int32(code_z) >> (2 * turn)) & 3
+        tile = lax.rem(y + ahead_y, ny) * nz + lax.rem(z + ahead_z, nz)
+
+        @pl.when(turn > 0)
         def _():
             pull_from(tile).wait_recv()
 
@@ -343,7 +395,7 @@
     next_flag, last_flag = flag(s < ns - 1), flag(s > 0)
     linked = next_flag + last_flag
     matched = mcount[...] * next_flag
-    gains = stiff[...]
+    gains = stiffv[...]
     inverse = RATE / (4.0 * gains + SPRING_SEC * linked + matched)
     pulled = [scat[0:side] + scat[side : 2 * side], scat[2 * side : 3 * side] + scat[3 * side :]]
     row_at = lax.broadcasted_iota(jnp.int32, (side, side), 0)
@@ -354,7 +406,7 @@
         for copy in swaps[turn]:
             copy.wait_recv()
         for channel in range(2):
-            value = disp[channel] if turn == 0 else ub[turn - 1, channel]
+            value = dispv[channel] if turn == 0 else ub[turn - 1, channel]
             lines = [halo[turn, at, channel : channel + 1, :] * flags[at] for at in range(4)]
             cols = [
                 jnp.sum(jnp.where(eye, jnp.broadcast_to(line, (side, side)), 0.0), axis=1, keepdims=True)
@@ -366,16 +418,21 @@
             around += jnp.where(col_at == side - 1, cols[1], pltpu.roll(value, side - 1, 1))
             force = gains * (around - 4.0 * value) + pulled[channel] - matched * value
             force += SPRING_SEC * (
-                lob[turn, channel] * last_flag + upb[turn, channel] * next_flag - linked * value
+                lob[turn, channel].astype(jnp.float32) * last_flag
+                + upb[turn, channel].astype(jnp.float32) * next_flag
+                - linked * value
             )
             moved = value + force * inverse
             if turn == ITERS - 1:
                 out[channel] = moved
             else:
+                wire[turn + 1, channel] = moved.astype(jnp.bfloat16)
+                for copy in swaps[turn + 1][4 + 2 * channel : 6 + 2 * channel]:
+                    copy.start()
                 ub[turn, channel] = moved
                 set_edges(turn + 1, channel, moved)
         if turn < ITERS - 1:
-            for copy in swaps[turn + 1]:
+            for copy in swaps[turn + 1][:4]:
                 copy.start()
 
     for copy in shift + tables + queries + keys + partials + [c for swap in swaps for c in swap]:
@@ -394,7 +451,7 @@
 
     def per_device(desc, pos, ids, blocks, count, disp, stiff):
         desc, pos, ids = desc[0, 0, 0], pos[0, 0, 0], ids[0, 0]
-        blocks, count = blocks[0, 0, 0], count.reshape(1)
+        blocks = blocks[0, 0, 0]
         disp, stiff = disp[0], stiff[0]
         pts, feat = desc.shape
         side = stiff.shape[0]
@@ -407,9 +464,12 @@
         moved = pl.pallas_call(
             functools.partial(kernel, (ns, ny, nz, blocks.shape[0])),
             out_shape=jax.ShapeDtypeStruct(disp.shape, f32),
-            in_specs=[smem, smem] + [vmem] * 5,
+            in_specs=[smem, smem] + [pl.BlockSpec(memory_space=pl.ANY)] * 5,
             out_specs=vmem,
             scratch_shapes=[
+                pltpu.VMEM((2, side, side), f32),
+                pltpu.VMEM((side, side), f32),
+                pltpu.VMEM((2, pts), bf16),
                 pltpu.VMEM((4, pts, feat), bf16),
                 tile, tile, tile, tile,
                 pltpu.VMEM((4, 2, pts), bf16),
@@ -423,14 +483,19 @@
                 pltpu.VMEM((side, side), f32),
                 pltpu.VMEM((4, 16, pts), f32),
                 pltpu.VMEM((4, 1, pts), f32),
+                pltpu.VMEM((CAPB * BLK, pts), f32),
+                pltpu.VMEM((CAPB * BLK, pts), f32),
+                pltpu.VMEM((CAPB, 1, pts), f32),
+                pltpu.VMEM((CAPB, 1, pts), f32),
                 pltpu.VMEM((4, 4, pts), f32),
                 pltpu.VMEM((4, 4, pts), f32),
                 pltpu.VMEM((2, pts), f32),
                 pltpu.VMEM((plane, 2, pts), f32),
                 pltpu.VMEM((4 * side, side), f32),
                 pltpu.VMEM((ITERS - 1, 2, side, side), f32),
-                pltpu.VMEM((ITERS, 2, side, side), f32),
-                pltpu.VMEM((ITERS, 2, side, side), f32),
+                pltpu.VMEM((ITERS, 2, side, side), bf16),
+                pltpu.VMEM((ITERS, 2, side, side), bf16),
+                pltpu.VMEM((ITERS, 2, side, side), bf16),
                 pltpu.VMEM((ITERS, 4, 2, side), f32),
                 pltpu.VMEM((ITERS, 4, 2, side), f32),
                 dma((6,)), dma((6,)),
@@ -440,7 +505,8 @@
                 dma((plane,)), dma((plane,)),
                 dma((plane,)), dma((plane,)),
                 dma((3,)), dma((3,)),
-                dma((ITERS, 6)), dma((ITERS, 6)),
+                dma((ITERS, 8)), dma((ITERS, 8)),
+                dma((5,)), pltpu.SemaphoreType.REGULAR((3,)),
             ],
             compiler_params=pltpu.CompilerParams(
                 collective_id=0, has_side_effects=True, vmem_limit_bytes=56 * 1024 * 1024

time: 99.4 us -> 79.5 us (0.80)
  Pallas kernels: 96.7 us -> 77.2 us
    pallas_call x1, Pallas kernels: 96.7 us -> 77.2 us  [per_device(): pl.pallas_call(functools.partial(kernel, (ns, ny, nz, blocks.shape[0])),...]
where the time goes in v2:
time: 79.5 us; the launch traced here: 79.4 us
  Pallas kernels  77.2 us (97%)
  local copies, waits for them, and re-layouts  1.57 us (2%)
    pallas_call x1, Pallas kernels, per_device(): pl.pallas_call(functools.partial(kernel, (ns, ny, nz, blocks.shape[0])),...  77.2 us

profile of v2, /device:TPU:4, one launch (start us, length us, event | category | flops | bytes accessed | tf_op | source)
XLA Modules:
  0.0 79.4 jit_solution(10604603308350199382)
XLA Ops:
  0.7 77.2 %shard_map.73 = f32[2,128,128]{2,1,0:T(8,128)} custom-call(s32[32]{0:T(128)} %bitcast.13, s32[1,1,1]{2,1,0:T(1,128)S(6)} %copy.9.count_ref, bf16[1024,128]{1,0:T(8,128)(2,1)} %bitcast.8, bf16[2,1024]{1,0:T(2,128)(2,1)} %bitcast.11, s32[1,1024]{1,0:T(1,128)} %bitcast.12, f32[2,128,128]{2,1,0:T(8,128)} %bitcast.9, f32[128,128]{1,0:T(8,128)} %bitcast.10), custom_call_target="tpu_custom_call" | custom-call | tf_op jit(solution)/shard_map/pallas_call | solution.py:464
  77.8 1.6 %copy.10 = f32[1,2,128,128]{3,2,1,0:T(8,128)} copy(f32[1,2,128,128]{3,2,1,0:T(8,128)} %bitcast.7) | data formatting | bytes 262144

commit v3 on v2

--- a/solution.py
+++ b/solution.py
@@ -48,7 +48,7 @@
     sizes, list_ref, count_ref, desc, pos, ids, disp, stiff, out,
     dispv, stiffv, posv, qbuf, kin0, kin1, kin2, kin3, pin, kwork, vwork, tabv, tabs, idb, onea, onec, mcount,
     acc, mx, sbuf0, sbuf1, tops0, tops1, part, prt, pull, pbuf, scat, ub, wire, lob, upb, edge, halo,
-    qs, qr, hs, hr, ks, kr, ts, tr, tl, ids_s, ids_r, ps, pr, cs, cr, us, ur, ls, gossip,
+    qs, qr, hs, hr, ks, kr, ts, tr, tl, ids_s, ids_r, ps, pr, cs, cr, us, ur, ls,
 ):
     ns, ny, nz, slots = sizes
     plane = ny * nz
@@ -99,15 +99,30 @@
     tables = [
         remote(tabv.at[0], tabv.at[1], ts.at[0], tr.at[0], right),
         remote(tabv.at[0], tabv.at[2], ts.at[1], tr.at[1], left),
-        remote(tabv.at[0], tabv.at[3], ts.at[2], tr.at[2], across),
-    ]
-    queries = [
-        remote(desc.at[rows[0]], qbuf.at[1, rows[0]], qs.at[0], qr.at[0], right),
-        remote(desc.at[rows[1]], qbuf.at[2, rows[1]], qs.at[1], qr.at[1], left),
-        remote(desc.at[rows[1]], qbuf.at[1, rows[1]], qs.at[2], qr.at[2], right),
-        remote(desc.at[rows[0]], qbuf.at[2, rows[0]], qs.at[3], qr.at[3], left),
-        remote(qbuf.at[1, rows[0]], qbuf.at[3, rows[0]], qs.at[4], qr.at[4], right),
-        remote(qbuf.at[2, rows[1]], qbuf.at[3, rows[1]], qs.at[5], qr.at[5], left),
+        remote(tabv.at[1], tabv.at[3], ts.at[2], tr.at[2], right),
+    ]
+    piece = [pl.ds(at * CHUNK, CHUNK) for at in range(pts // CHUNK)]
+    to_right = [remote(desc.at[piece[at]], qbuf.at[1, piece[at]], qs.at[at], qr.at[at], right) for at in range(4)]
+    to_left = [
+        remote(desc.at[piece[at]], qbuf.at[2, piece[at]], qs.at[4 + at], qr.at[4 + at], left)
+        for at in (2, 3, 0, 1)
+    ]
+    on_right = [
+        remote(qbuf.at[1, piece[at]], qbuf.at[3, piece[at]], qs.at[8 + at], qr.at[8 + at], right) for at in (0, 1)
+    ]
+    on_left = [
+        remote(qbuf.at[2, piece[at]], qbuf.at[3, piece[at]], qs.at[8 + at], qr.at[8 + at], left) for at in (2, 3)
+    ]
+    queries = to_right + to_left + on_right + on_left
+    lefts = y * nz + lax.rem(z + nz - 1, nz)
+    row, row_up = pl.ds(y * nz, nz), pl.ds(lax.rem(y + ny - 1, ny) * nz, nz)
+    names = [
+        remote(ids, idb.at[me], ids_s.at[0], ids_r.at[0], right),
+        remote(ids, idb.at[me], ids_s.at[1], ids_r.at[1], left),
+        remote(idb.at[lefts], idb.at[lefts], ids_s.at[2], ids_r.at[2], right),
+        remote(idb.at[row], idb.at[row], ids_s.at[3], ids_r.at[3], down),
+        remote(idb.at[row], idb.at[row], ids_s.at[4], ids_r.at[4], up),
+        remote(idb.at[row_up], idb.at[row_up], ids_s.at[5], ids_r.at[5], down),
     ]
     keys = [
         remote(kin0.at[rows[0]], kin1.at[rows[0]], ks.at[0], kr.at[0], down),
@@ -140,13 +155,6 @@
 
     swaps = [exchange(turn) for turn in range(ITERS)]
 
-    def ids_copy(by):
-        _, device = peer(by)
-        return remote(ids, idb.at[me], ids_s.at[by], ids_r.at[me], device)
-
-    def ids_from(tile):
-        return remote(ids, idb.at[tile], ids_s.at[0], ids_r.at[tile], before)
-
     def pull_copy(by):
         _, device = peer(by)
         return remote(pull, pbuf.at[me], ps.at[by], pr.at[me], device)
@@ -154,20 +162,11 @@
     def pull_from(tile):
         return remote(pull, pbuf.at[tile], ps.at[0], pr.at[tile], before)
 
-    def start_ids(by, carry):
-        ids_copy(by).start()
-        return carry
-
-    for copy in shift[:2] + tables[:2] + queries[:2] + shift[2:]:
+    for copy in shift + tables[:2] + names[:2]:
         copy.start()
-    for at, pair in enumerate(((right, left), (down, up), (down, up))):
-        for device in pair:
-            pl.semaphore_signal(gossip.at[at], inc=1, device_id=device, device_id_type=MESH)
-        pl.semaphore_wait(gossip.at[at], 2)
-    lax.fori_loop(1, plane, start_ids, 0)
-    tables[2].start()
-    for copy in queries[2:4]:
-        copy.start()
+    for at in range(3):
+        to_right[at].start()
+        to_left[at].start()
     for copy in loads:
         copy.wait()
 
@@ -194,12 +193,19 @@
         set_edges(0, channel, dispv[channel])
         wire[0, channel] = dispv[channel].astype(jnp.bfloat16)
 
-    def one_hots(by, carry):
-        tile, _ = peer(by)
-
-        @pl.when(by > 0)
-        def _():
-            ids_from(tile).wait_recv()
+    order = [(0, 0), (1, 0), (3, 0), (2, 0), (0, 1), (0, 3), (1, 1), (3, 1), (1, 3), (3, 3)]
+    order += [(2, 1), (2, 3), (0, 2), (1, 2), (3, 2), (2, 2)]
+    wrap = lambda value: value - (1 << 32) if value >= 1 << 31 else value
+    code_y = wrap(sum(dy << (2 * at) for at, (dy, _) in enumerate(order)))
+    code_z = wrap(sum(dz << (2 * at) for at, (_, dz) in enumerate(order)))
+
+    def nearest(turn):
+        ahead_y = (jnp.int32(code_y) >> (2 * turn)) & 3
+        ahead_z = (jnp.int32(code_z) >> (2 * turn)) & 3
+        return lax.rem(y + ahead_y, ny) * nz + lax.rem(z + ahead_z, nz)
+
+    def one_hots(turn, carry):
+        tile = nearest(turn)
 
         vertex = idb[tile]
         level = lax.broadcasted_iota(jnp.int32, (side, pts), 0)
@@ -214,116 +220,151 @@
 
     factor = 16.0 / feat * math.log2(math.e)
 
-    def found(step):
-        q, k = lax.div(step, 4), lax.rem(step, 4)
-        key_row = lax.rem(y + jnp.where(k == 1, ny - 1, jnp.where(k == 2, 1, jnp.where(k == 3, 2, 0))), ny)
-        lane = (key_row * nz + z) * 8
-        codes = [tabs[q, slot, lane] for slot in range(CAPB)]
-        return q, k, [code & (blocks - 1) for code in codes], [code < blocks for code in codes]
-
-    chunks = [pl.ds(at * CHUNK, CHUNK) for at in range(pts // CHUNK)]
-
-    def scorer(step, sbuf, tops):
-        q, k, at_block, live = found(step)
+    def packed(values, at):
+        return (jnp.int32(sum(value << (2 * i) for i, value in enumerate(values))) >> (2 * at)) & 3
+
+    def unit(step):
+        early = step < 16
+        quarter, rest = lax.div(step, 4), lax.rem(step, 4)
+        pair, k = jnp.where(early, rest, quarter), jnp.where(early, quarter, rest)
+        parts = []
+        for slots, places in (
+            ((0, 0, 1, 1, 1, 3, 3, 1), (0, 2, 0, 1, 2, 0, 1, 3)),
+            ((0, 0, 2, 2, 2, 3, 3, 2), (1, 3, 2, 3, 0, 2, 3, 1)),
+        ):
+            q = packed(slots, pair)
+            start = pl.multiple_of(packed(places, pair) * CHUNK, CHUNK)
+            key_row = lax.rem(y + packed((0, ny - 1, 1, 2), k), ny)
+            lane = (key_row * nz + z) * 8
+            codes = [tabs[q, slot, lane] for slot in range(CAPB)]
+            parts.append(
+                (q, k, pl.ds(start, CHUNK), [code & (blocks - 1) for code in codes], [code < blocks for code in codes])
+            )
+        return parts
+
+    def score(part_at, sbuf, tops, at):
+        q, k, cols, at_block, live = part_at
         key_rows = jnp.concatenate([kwork[k, block] for block in at_block], axis=0)
-
-        def score(cols):
-            raw = lax.dot_general(key_rows, qbuf[q, cols, :], NT, preferred_element_type=jnp.float32)
-            sbuf[:, cols] = raw
-            for i in range(CAPB):
-                top = jnp.max(raw[i * BLK : (i + 1) * BLK], axis=0, keepdims=True)
-                tops[i, :, cols] = jnp.where(live[i], top, NEG)
-
-        return score
-
-    def weigher(step, sbuf, tops):
-        q, k, at_block, live = found(step)
+        raw = lax.dot_general(key_rows, qbuf[q, cols, :], NT, preferred_element_type=jnp.float32)
+        sbuf[at] = raw
+        for i in range(CAPB):
+            top = jnp.max(raw[i * BLK : (i + 1) * BLK], axis=0, keepdims=True)
+            tops[at, i] = jnp.where(live[i], top, NEG)
+
+    def weigh(part_at, sbuf, tops, at):
+        q, k, cols, at_block, live = part_at
         values = jnp.concatenate([vwork[k, block] for block in at_block], axis=1)
-
-        def weigh(cols):
-            old = mx[q, :, cols]
-            new = functools.reduce(jnp.maximum, [tops[i, :, cols] for i in range(CAPB)], old)
-            weights = []
-            for i in range(CAPB):
-                base = jnp.where(live[i], new, -NEG)
-                raw = sbuf[i * BLK : (i + 1) * BLK, cols]
-                weights.append(jnp.exp2((raw - base) * factor).astype(jnp.bfloat16))
-            added = lax.dot_general(
-                values, jnp.concatenate(weights, axis=0), NN, preferred_element_type=jnp.float32
-            )
-            acc[q, :, cols] = acc[q, :, cols] * jnp.exp2((old - new) * factor) + added
-            mx[q, :, cols] = new
-
-        return weigh
+        old = mx[q, :, cols]
+        new = functools.reduce(jnp.maximum, [tops[at, i] for i in range(CAPB)], old)
+        weights = []
+        for i in range(CAPB):
+            base = jnp.where(live[i], new, -NEG)
+            raw = sbuf[at, i * BLK : (i + 1) * BLK, :]
+            weights.append(jnp.exp2((raw - base) * factor).astype(jnp.bfloat16))
+        added = lax.dot_general(values, jnp.concatenate(weights, axis=0), NN, preferred_element_type=jnp.float32)
+        acc[q, :, cols] = acc[q, :, cols] * jnp.exp2((old - new) * factor) + added
+        mx[q, :, cols] = new
+
+    def load_table(slot):
+        local = pltpu.make_async_copy(tabv.at[slot], tabs.at[slot], tl.at[slot])
+        local.start()
+        local.wait()
+
+    def settle(slot):
+        part[slot, 0:3, :] = acc[slot, 0:3, :]
+        part[slot, 3:4, :] = mx[slot]
 
     def match(step, carry):
-        @pl.when(step == 0)
-        def _():
-            queries[0].wait_recv()
-            queries[4].start()
-            queries[1].wait_recv()
-            queries[5].start()
+        @pl.when(step == 1)
+        def _():
             keys[0].wait_recv()
             keys[4].start()
             keys[1].wait_recv()
             keys[5].start()
             keys[6].wait_recv()
             keys[8].start()
-            lax.fori_loop(0, plane, one_hots, 0)
+            to_right[0].wait_recv()
+            on_right[0].start()
+            to_left[0].wait_recv()
+            on_left[0].start()
+            for slot in (1, 2):
+                tables[slot - 1].wait_recv()
+                load_table(slot)
+            tables[2].start()
+            names[0].wait_recv()
+            names[2].start()
+
+        @pl.when(step == 2)
+        def _():
+            to_right[1].wait_recv()
+            on_right[1].start()
+            to_left[1].wait_recv()
+            on_left[1].start()
+            to_right[3].start()
+            to_left[3].start()
+
+        @pl.when(step == 3)
+        def _():
             keys[2].wait_recv()
             set_key(1, kin1)
 
-        @pl.when(step == 1)
+        @pl.when(step == 7)
         def _():
             keys[3].wait_recv()
             keys[7].wait_recv()
             set_key(2, kin2)
 
-        @pl.when(step == 2)
+        @pl.when(step == 11)
         def _():
             keys[4].wait_recv()
             keys[5].wait_recv()
             keys[8].wait_recv()
             set_key(3, kin3)
 
-        for slot in range(1, 4):
-
-            @pl.when(step == 4 * slot - 1)
-            def _():
-                for copy in ((), (2,), (3,), (4, 5))[slot]:
-                    queries[copy].wait_recv()
-                tables[slot - 1].wait_recv()
-                local = pltpu.make_async_copy(tabv.at[slot], tabs.at[slot], tl.at[slot])
-                local.start()
-                local.wait()
-
-        @pl.when(step == 10)
-        def _():
+        @pl.when(step == 15)
+        def _():
+            to_right[2].wait_recv()
+            to_left[2].wait_recv()
+            names[1].wait_recv()
+            names[2].wait_recv()
+            names[3].start()
+            names[4].start()
+
+        @pl.when(step == 19)
+        def _():
+            on_right[0].wait_recv()
+            on_left[0].wait_recv()
+            tables[2].wait_recv()
+            load_table(3)
+
+        @pl.when(step == 23)
+        def _():
+            on_right[1].wait_recv()
+            on_left[1].wait_recv()
+            names[3].wait_recv()
+            names[5].start()
             for copy in swaps[0]:
                 copy.start()
 
-        following = lax.rem(step + 1, 16)
+        @pl.when(step == 27)
+        def _():
+            to_right[3].wait_recv()
+            to_left[3].wait_recv()
+
         for parity, first, second in ((0, (sbuf0, tops0), (sbuf1, tops1)), (1, (sbuf1, tops1), (sbuf0, tops0))):
 
             @pl.when(lax.rem(step, 2) == parity)
             def _():
-                score, weigh = scorer(following, *second), weigher(step, *first)
-                for cols in chunks:
-                    weigh(cols)
-                    score(cols)
-
-        q, k = lax.div(step, 4), lax.rem(step, 4)
-
-        @pl.when(k == 3)
-        def _():
-            part[q, 0:3, :] = acc[q, 0:3, :]
-            part[q, 3:4, :] = mx[q]
-
-        for slot in range(1, 4):
-
-            @pl.when(step == 4 * slot + 3)
-            def _():
-                partials[slot - 1].start()
+                ahead, here = unit(lax.rem(step + 1, 32)), unit(step)
+                for at in range(2):
+                    score(ahead[at], *second, at)
+                for at in range(2):
+                    weigh(here[at], *first, at)
+
+        @pl.when(step == 27)
+        def _():
+            settle(3)
+            partials[2].start()
 
         return carry
 
@@ -340,10 +381,16 @@
     keys[6].start()
     keys[7].start()
     set_key(0, kin0)
-    score = scorer(jnp.int32(0), sbuf0, tops0)
-    for cols in chunks:
-        score(cols)
-    lax.fori_loop(0, 16, match, 0)
+    for at, part_at in enumerate(unit(jnp.int32(0))):
+        score(part_at, sbuf0, tops0, at)
+    lax.fori_loop(0, 32, match, 0)
+    for slot in (1, 2):
+        settle(slot)
+        partials[slot - 1].start()
+    settle(0)
+    names[4].wait_recv()
+    names[5].wait_recv()
+    lax.fori_loop(0, plane // 2, one_hots, 0)
 
     has_next = s < ns - 1
     for copy in partials:
@@ -361,17 +408,10 @@
 
     lax.fori_loop(1, plane, start_pull, 0)
     pbuf[pl.ds(me, 1)] = pull[...][None]
-
-    order = [(0, 0), (1, 0), (3, 0), (2, 0), (0, 1), (0, 3), (1, 1), (3, 1), (1, 3), (3, 3)]
-    order += [(2, 1), (2, 3), (0, 2), (1, 2), (3, 2), (2, 2)]
-    wrap = lambda value: value - (1 << 32) if value >= 1 << 31 else value
-    code_y = wrap(sum(dy << (2 * at) for at, (dy, _) in enumerate(order)))
-    code_z = wrap(sum(dz << (2 * at) for at, (_, dz) in enumerate(order)))
+    lax.fori_loop(plane // 2, plane, one_hots, 0)
 
     def gather_pull(turn, carry):
-        ahead_y = (jnp.int32(code_y) >> (2 * turn)) & 3
-        ahead_z = (jnp.int32(code_z) >> (2 * turn)) & 3
-        tile = lax.rem(y + ahead_y, ny) * nz + lax.rem(z + ahead_z, nz)
+        tile = nearest(turn)
 
         @pl.when(turn > 0)
         def _():
@@ -435,11 +475,10 @@
             for copy in swaps[turn + 1][:4]:
                 copy.start()
 
-    for copy in shift + tables + queries + keys + partials + [c for swap in swaps for c in swap]:
+    for copy in shift + tables + names + queries + keys + partials + [c for swap in swaps for c in swap]:
         copy.wait_send()
 
     def finish(by, carry):
-        ids_copy(by).wait_send()
         pull_copy(by).wait_send()
         return carry
 
@@ -483,10 +522,10 @@
                 pltpu.VMEM((side, side), f32),
                 pltpu.VMEM((4, 16, pts), f32),
                 pltpu.VMEM((4, 1, pts), f32),
-                pltpu.VMEM((CAPB * BLK, pts), f32),
-                pltpu.VMEM((CAPB * BLK, pts), f32),
-                pltpu.VMEM((CAPB, 1, pts), f32),
-                pltpu.VMEM((CAPB, 1, pts), f32),
+                pltpu.VMEM((2, CAPB * BLK, CHUNK), f32),
+                pltpu.VMEM((2, CAPB * BLK, CHUNK), f32),
+                pltpu.VMEM((2, CAPB, 1, CHUNK), f32),
+                pltpu.VMEM((2, CAPB, 1, CHUNK), f32),
                 pltpu.VMEM((4, 4, pts), f32),
                 pltpu.VMEM((4, 4, pts), f32),
                 pltpu.VMEM((2, pts), f32),
@@ -498,15 +537,15 @@
                 pltpu.VMEM((ITERS, 2, side, side), bf16),
                 pltpu.VMEM((ITERS, 4, 2, side), f32),
                 pltpu.VMEM((ITERS, 4, 2, side), f32),
-                dma((6,)), dma((6,)),
+                dma((12,)), dma((12,)),
                 dma((3,)), dma((3,)),
                 dma((9,)), dma((9,)),
                 dma((3,)), dma((3,)), dma((4,)),
-                dma((plane,)), dma((plane,)),
+                dma((6,)), dma((6,)),
                 dma((plane,)), dma((plane,)),
                 dma((3,)), dma((3,)),
                 dma((ITERS, 8)), dma((ITERS, 8)),
-                dma((5,)), pltpu.SemaphoreType.REGULAR((3,)),
+                dma((5,)),
             ],
             compiler_params=pltpu.CompilerParams(
                 collective_id=0, has_side_effects=True, vmem_limit_bytes=56 * 1024 * 1024

time: 79.5 us -> 70.9 us (0.89)
  Pallas kernels: 77.2 us -> 68.5 us
    pallas_call x1, Pallas kernels: 77.2 us -> 68.5 us  [per_device(): pl.pallas_call(functools.partial(kernel, (ns, ny, nz, blocks.shape[0])),...]
where the time goes in v3:
time: 70.9 us; the launch traced here: 70.7 us
  Pallas kernels  68.5 us (97%)
  local copies, waits for them, and re-layouts  1.57 us (2%)
    pallas_call x1, Pallas kernels, per_device(): pl.pallas_call(functools.partial(kernel, (ns, ny, nz, blocks.shape[0])),...  68.5 us
    unnamed x1, local copies, waits for them, and re-layouts  1.57 us

profile of v3, /device:TPU:4, one launch (start us, length us, event | category | flops | bytes accessed | tf_op | source)
XLA Modules:
  0.0 70.7 jit_solution(3029675034427823481)
XLA Ops:
  0.7 68.5 %shard_map.73 = f32[2,128,128]{2,1,0:T(8,128)} custom-call(s32[32]{0:T(128)} %bitcast.13, s32[1,1,1]{2,1,0:T(1,128)S(6)} %copy.9.count_ref, bf16[1024,128]{1,0:T(8,128)(2,1)} %bitcast.8, bf16[2,1024]{1,0:T(2,128)(2,1)} %bitcast.11, s32[1,1024]{1,0:T(1,128)} %bitcast.12, f32[2,128,128]{2,1,0:T(8,128)} %bitcast.9, f32[128,128]{1,0:T(8,128)} %bitcast.10), custom_call_target="tpu_custom_call" | custom-call | tf_op jit(solution)/shard_map/pallas_call | solution.py:503
  69.1 1.6 %copy.10 = f32[1,2,128,128]{3,2,1,0:T(8,128)} copy(f32[1,2,128,128]{3,2,1,0:T(8,128)} %bitcast.7) | data formatting | bytes 262144

commit v4 on v3

--- a/solution.py
+++ b/solution.py
@@ -47,7 +47,7 @@
 def kernel(
     sizes, list_ref, count_ref, desc, pos, ids, disp, stiff, out,
     dispv, stiffv, posv, qbuf, kin0, kin1, kin2, kin3, pin, kwork, vwork, tabv, tabs, idb, onea, onec, mcount,
-    acc, mx, sbuf0, sbuf1, tops0, tops1, part, prt, pull, pbuf, scat, ub, wire, lob, upb, edge, halo,
+    acc, mx, sbuf0, sbuf1, tops0, tops1, part, prt, pull, pbuf, scat, coef, base, force, ub, first_below, first_above, wire, lob, upb, edge, halo,
     qs, qr, hs, hr, ks, kr, ts, tr, tl, ids_s, ids_r, ps, pr, cs, cr, us, ur, ls,
 ):
     ns, ny, nz, slots = sizes
@@ -142,15 +142,23 @@
     ]
 
     def exchange(turn):
+        if turn == 0:
+            source, below, above = (
+                [ref.at[channel] for channel in range(2)] for ref in (dispv, first_below, first_above)
+            )
+        else:
+            source, below, above = (
+                [ref.at[turn - 1, channel] for channel in range(2)] for ref in (wire, lob, upb)
+            )
         return [
             remote(edge.at[turn, 0], halo.at[turn, 1], us.at[turn, 0], ur.at[turn, 0], up),
             remote(edge.at[turn, 1], halo.at[turn, 0], us.at[turn, 1], ur.at[turn, 1], down),
             remote(edge.at[turn, 2], halo.at[turn, 3], us.at[turn, 2], ur.at[turn, 2], left),
             remote(edge.at[turn, 3], halo.at[turn, 2], us.at[turn, 3], ur.at[turn, 3], right),
-            remote(wire.at[turn, 0], lob.at[turn, 0], us.at[turn, 4], ur.at[turn, 4], after),
-            remote(wire.at[turn, 0], upb.at[turn, 0], us.at[turn, 5], ur.at[turn, 5], before),
-            remote(wire.at[turn, 1], lob.at[turn, 1], us.at[turn, 6], ur.at[turn, 6], after),
-            remote(wire.at[turn, 1], upb.at[turn, 1], us.at[turn, 7], ur.at[turn, 7], before),
+            remote(source[0], below[0], us.at[turn, 4], ur.at[turn, 4], after),
+            remote(source[0], above[0], us.at[turn, 5], ur.at[turn, 5], before),
+            remote(source[1], below[1], us.at[turn, 6], ur.at[turn, 6], after),
+            remote(source[1], above[1], us.at[turn, 7], ur.at[turn, 7], before),
         ]
 
     swaps = [exchange(turn) for turn in range(ITERS)]
@@ -191,7 +199,6 @@
 
     for channel in range(2):
         set_edges(0, channel, dispv[channel])
-        wire[0, channel] = dispv[channel].astype(jnp.bfloat16)
 
     order = [(0, 0), (1, 0), (3, 0), (2, 0), (0, 1), (0, 3), (1, 1), (3, 1), (1, 3), (3, 3)]
     order += [(2, 1), (2, 3), (0, 2), (1, 2), (3, 2), (2, 2)]
@@ -224,22 +231,22 @@
         return (jnp.int32(sum(value << (2 * i) for i, value in enumerate(values))) >> (2 * at)) & 3
 
     def unit(step):
-        early = step < 16
-        quarter, rest = lax.div(step, 4), lax.rem(step, 4)
-        pair, k = jnp.where(early, rest, quarter), jnp.where(early, quarter, rest)
+        early = step < 8
+        high, low = lax.div(step, 2), lax.rem(step, 2)
         parts = []
-        for slots, places in (
-            ((0, 0, 1, 1, 1, 3, 3, 1), (0, 2, 0, 1, 2, 0, 1, 3)),
-            ((0, 0, 2, 2, 2, 3, 3, 2), (1, 3, 2, 3, 0, 2, 3, 1)),
-        ):
-            q = packed(slots, pair)
-            start = pl.multiple_of(packed(places, pair) * CHUNK, CHUNK)
-            key_row = lax.rem(y + packed((0, ny - 1, 1, 2), k), ny)
-            lane = (key_row * nz + z) * 8
-            codes = [tabs[q, slot, lane] for slot in range(CAPB)]
-            parts.append(
-                (q, k, pl.ds(start, CHUNK), [code & (blocks - 1) for code in codes], [code < blocks for code in codes])
-            )
+        for i in range(2):
+            pair, k = jnp.where(early, 2 * low + i, high), jnp.where(early, high, 2 * low + i)
+            for slots, places in (
+                ((0, 0, 1, 1, 1, 3, 3, 1), (0, 2, 0, 1, 2, 0, 1, 3)),
+                ((0, 0, 2, 2, 2, 3, 3, 2), (1, 3, 2, 3, 0, 2, 3, 1)),
+            ):
+                q = packed(slots, pair)
+                start = pl.multiple_of(packed(places, pair) * CHUNK, CHUNK)
+                key_row = lax.rem(y + packed((0, ny - 1, 1, 2), k), ny)
+                lane = (key_row * nz + z) * 8
+                codes = [tabs[q, slot, lane] for slot in range(CAPB)]
+                found = [code & (blocks - 1) for code in codes]
+                parts.append((q, k, pl.ds(start, CHUNK), found, [code < blocks for code in codes]))
         return parts
 
     def score(part_at, sbuf, tops, at):
@@ -275,7 +282,7 @@
         part[slot, 3:4, :] = mx[slot]
 
     def match(step, carry):
-        @pl.when(step == 1)
+        @pl.when(step == 0)
         def _():
             keys[0].wait_recv()
             keys[4].start()
@@ -294,8 +301,6 @@
             names[0].wait_recv()
             names[2].start()
 
-        @pl.when(step == 2)
-        def _():
             to_right[1].wait_recv()
             on_right[1].start()
             to_left[1].wait_recv()
@@ -303,25 +308,25 @@
             to_right[3].start()
             to_left[3].start()
 
-        @pl.when(step == 3)
+        @pl.when(step == 1)
         def _():
             keys[2].wait_recv()
             set_key(1, kin1)
 
-        @pl.when(step == 7)
+        @pl.when(step == 3)
         def _():
             keys[3].wait_recv()
             keys[7].wait_recv()
             set_key(2, kin2)
 
-        @pl.when(step == 11)
+        @pl.when(step == 5)
         def _():
             keys[4].wait_recv()
             keys[5].wait_recv()
             keys[8].wait_recv()
             set_key(3, kin3)
 
-        @pl.when(step == 15)
+        @pl.when(step == 7)
         def _():
             to_right[2].wait_recv()
             to_left[2].wait_recv()
@@ -330,14 +335,14 @@
             names[3].start()
             names[4].start()
 
-        @pl.when(step == 19)
+        @pl.when(step == 9)
         def _():
             on_right[0].wait_recv()
             on_left[0].wait_recv()
             tables[2].wait_recv()
             load_table(3)
 
-        @pl.when(step == 23)
+        @pl.when(step == 11)
         def _():
             on_right[1].wait_recv()
             on_left[1].wait_recv()
@@ -346,7 +351,7 @@
             for copy in swaps[0]:
                 copy.start()
 
-        @pl.when(step == 27)
+        @pl.when(step == 13)
         def _():
             to_right[3].wait_recv()
             to_left[3].wait_recv()
@@ -355,13 +360,13 @@
 
             @pl.when(lax.rem(step, 2) == parity)
             def _():
-                ahead, here = unit(lax.rem(step + 1, 32)), unit(step)
-                for at in range(2):
+                ahead, here = unit(step + 1), unit(step)
+                for at in range(4):
                     score(ahead[at], *second, at)
-                for at in range(2):
+                for at in range(4):
                     weigh(here[at], *first, at)
 
-        @pl.when(step == 27)
+        @pl.when(step == 13)
         def _():
             settle(3)
             partials[2].start()
@@ -383,7 +388,9 @@
     set_key(0, kin0)
     for at, part_at in enumerate(unit(jnp.int32(0))):
         score(part_at, sbuf0, tops0, at)
-    lax.fori_loop(0, 32, match, 0)
+    lax.fori_loop(0, 15, match, 0)
+    for at, part_at in enumerate(unit(jnp.int32(15))):
+        weigh(part_at, sbuf1, tops1, at)
     for slot in (1, 2):
         settle(slot)
         partials[slot - 1].start()
@@ -410,6 +417,39 @@
     pbuf[pl.ds(me, 1)] = pull[...][None]
     lax.fori_loop(plane // 2, plane, one_hots, 0)
 
+    flag = lambda test: jnp.where(test, 1.0, 0.0)
+    next_flag, last_flag = flag(s < ns - 1), flag(s > 0)
+    row_at = lax.broadcasted_iota(jnp.int32, (side, side), 0)
+    col_at = lax.broadcasted_iota(jnp.int32, (side, side), 1)
+    flags = [flag(y > 0), flag(y < ny - 1), flag(z > 0), flag(z < nz - 1)]
+    coef[0] = RATE / (4.0 * stiffv[...] + SPRING_SEC * (next_flag + last_flag) + mcount[...] * next_flag)
+    coef[1] = coef[0] * stiffv[...]
+
+    def inside(value):
+        around = jnp.where(row_at == 0, 0.0, pltpu.roll(value, 1, 0))
+        around += jnp.where(row_at == side - 1, 0.0, pltpu.roll(value, side - 1, 0))
+        around += jnp.where(col_at == 0, 0.0, pltpu.roll(value, 1, 1))
+        around += jnp.where(col_at == side - 1, 0.0, pltpu.roll(value, side - 1, 1))
+        return (1.0 - RATE) * value + coef[1] * around
+
+    def outside(turn, channel):
+        lines = [halo[turn, at, channel : channel + 1, :] * flags[at] for at in range(4)]
+        cols = [
+            jnp.sum(jnp.where(eye, jnp.broadcast_to(line, (side, side)), 0.0), axis=1, keepdims=True)
+            for line in lines[2:]
+        ]
+        edges = jnp.where(row_at == 0, lines[0], 0.0) + jnp.where(row_at == side - 1, lines[1], 0.0)
+        edges += jnp.where(col_at == 0, cols[0], 0.0) + jnp.where(col_at == side - 1, cols[1], 0.0)
+        below = first_below[channel] if turn == 0 else lob[turn - 1, channel].astype(jnp.float32)
+        above = first_above[channel] if turn == 0 else upb[turn - 1, channel].astype(jnp.float32)
+        stack = below * (SPRING_SEC * last_flag) + above * (SPRING_SEC * next_flag)
+        return coef[1] * edges + coef[0] * stack
+
+    for copy in swaps[0]:
+        copy.wait_recv()
+    for channel in range(2):
+        base[channel] = inside(dispv[channel]) + outside(0, channel)
+
     def gather_pull(turn, carry):
         tile = nearest(turn)
 
@@ -420,53 +460,36 @@
         row_hot = onea[tile].reshape(side // 16, 16, pts)
         pieces = []
         for channel in range(2):
-            value = jnp.broadcast_to(pbuf[tile, channel : channel + 1, :], (16, pts))
-            high = value.astype(jnp.bfloat16)
-            low = (value - high.astype(jnp.float32)).astype(jnp.bfloat16)
-            for piece in (high, low):
-                pieces.append((row_hot * piece[None]).reshape(side, pts))
+            value = jnp.broadcast_to(pbuf[tile, channel : channel + 1, :], (16, pts)).astype(jnp.bfloat16)
+            pieces.append((row_hot * value[None]).reshape(side, pts))
         stacked = jnp.concatenate(pieces, axis=0)
         scat[...] += lax.dot_general(stacked, onec[tile], NT, preferred_element_type=jnp.float32)
         return carry
 
     lax.fori_loop(0, plane, gather_pull, 0)
 
-    flag = lambda test: jnp.where(test, 1.0, 0.0)
-    next_flag, last_flag = flag(s < ns - 1), flag(s > 0)
-    linked = next_flag + last_flag
-    matched = mcount[...] * next_flag
-    gains = stiffv[...]
-    inverse = RATE / (4.0 * gains + SPRING_SEC * linked + matched)
-    pulled = [scat[0:side] + scat[side : 2 * side], scat[2 * side : 3 * side] + scat[3 * side :]]
-    row_at = lax.broadcasted_iota(jnp.int32, (side, side), 0)
-    col_at = lax.broadcasted_iota(jnp.int32, (side, side), 1)
-    flags = [flag(y > 0), flag(y < ny - 1), flag(z > 0), flag(z < nz - 1)]
-
+    pulled = [scat[0:side], scat[side:]]
+    for channel in range(2):
+        force[channel] = coef[0] * pulled[channel]
     for turn in range(ITERS):
-        for copy in swaps[turn]:
-            copy.wait_recv()
+        settled = []
         for channel in range(2):
-            value = dispv[channel] if turn == 0 else ub[turn - 1, channel]
-            lines = [halo[turn, at, channel : channel + 1, :] * flags[at] for at in range(4)]
-            cols = [
-                jnp.sum(jnp.where(eye, jnp.broadcast_to(line, (side, side)), 0.0), axis=1, keepdims=True)
-                for line in lines[2:]
-            ]
-            around = jnp.where(row_at == 0, lines[0], pltpu.roll(value, 1, 0))
-            around += jnp.where(row_at == side - 1, lines[1], pltpu.roll(value, side - 1, 0))
-            around += jnp.where(col_at == 0, cols[0], pltpu.roll(value, 1, 1))
-            around += jnp.where(col_at == side - 1, cols[1], pltpu.roll(value, side - 1, 1))
-            force = gains * (around - 4.0 * value) + pulled[channel] - matched * value
-            force += SPRING_SEC * (
-                lob[turn, channel].astype(jnp.float32) * last_flag
-                + upb[turn, channel].astype(jnp.float32) * next_flag
-                - linked * value
-            )
-            moved = value + force * inverse
+            if turn == 0:
+                settled.append(base[channel])
+            else:
+                settled.append(inside(ub[turn - 1, channel]) + force[channel])
+        if turn > 0:
+            for copy in swaps[turn]:
+                copy.wait_recv()
+        for channel in range(2):
+            if turn == 0:
+                moved = base[channel] + force[channel]
+            else:
+                moved = settled[channel] + outside(turn, channel)
             if turn == ITERS - 1:
                 out[channel] = moved
             else:
-                wire[turn + 1, channel] = moved.astype(jnp.bfloat16)
+                wire[turn, channel] = moved.astype(jnp.bfloat16)
                 for copy in swaps[turn + 1][4 + 2 * channel : 6 + 2 * channel]:
                     copy.start()
                 ub[turn, channel] = moved
@@ -522,19 +545,24 @@
                 pltpu.VMEM((side, side), f32),
                 pltpu.VMEM((4, 16, pts), f32),
                 pltpu.VMEM((4, 1, pts), f32),
-                pltpu.VMEM((2, CAPB * BLK, CHUNK), f32),
-                pltpu.VMEM((2, CAPB * BLK, CHUNK), f32),
-                pltpu.VMEM((2, CAPB, 1, CHUNK), f32),
-                pltpu.VMEM((2, CAPB, 1, CHUNK), f32),
+                pltpu.VMEM((4, CAPB * BLK, CHUNK), f32),
+                pltpu.VMEM((4, CAPB * BLK, CHUNK), f32),
+                pltpu.VMEM((4, CAPB, 1, CHUNK), f32),
+                pltpu.VMEM((4, CAPB, 1, CHUNK), f32),
                 pltpu.VMEM((4, 4, pts), f32),
                 pltpu.VMEM((4, 4, pts), f32),
                 pltpu.VMEM((2, pts), f32),
                 pltpu.VMEM((plane, 2, pts), f32),
-                pltpu.VMEM((4 * side, side), f32),
+                pltpu.VMEM((2 * side, side), f32),
+                pltpu.VMEM((2, side, side), f32),
+                pltpu.VMEM((2, side, side), f32),
+                pltpu.VMEM((2, side, side), f32),
                 pltpu.VMEM((ITERS - 1, 2, side, side), f32),
-                pltpu.VMEM((ITERS, 2, side, side), bf16),
-                pltpu.VMEM((ITERS, 2, side, side), bf16),
-                pltpu.VMEM((ITERS, 2, side, side), bf16),
+                pltpu.VMEM((2, side, side), f32),
+                pltpu.VMEM((2, side, side), f32),
+                pltpu.VMEM((ITERS - 1, 2, side, side), bf16),
+                pltpu.VMEM((ITERS - 1, 2, side, side), bf16),
+                pltpu.VMEM((ITERS - 1, 2, side, side), bf16),
                 pltpu.VMEM((ITERS, 4, 2, side), f32),
                 pltpu.VMEM((ITERS, 4, 2, side), f32),
                 dma((12,)), dma((12,)),

time: 70.9 us -> 66 us (0.931); the launches traced: 70.7 us -> 65 us
  Pallas kernels: 68.5 us -> 62.8 us
    pallas_call x1, Pallas kernels: 68.5 us -> 62.8 us  [per_device(): pl.pallas_call(functools.partial(kernel, (ns, ny, nz, blocks.shape[0])),...]
where the time goes in v4:
time: 66 us; the launch traced here: 65 us
  Pallas kernels  62.8 us (95%)
  local copies, waits for them, and re-layouts  1.57 us (2%)
  between operations  0.66 us (1%)
    pallas_call x1, Pallas kernels, per_device(): pl.pallas_call(functools.partial(kernel, (ns, ny, nz, blocks.shape[0])),...  62.8 us
    unnamed x1, local copies, waits for them, and re-layouts  1.57 us

profile of v4, /device:TPU:4, one launch (start us, length us, event | category | flops | bytes accessed | tf_op | source)
XLA Modules:
  0.0 65.0 jit_solution(1179319538383237526)
XLA Ops:
  0.7 62.8 %shard_map.73 = f32[2,128,128]{2,1,0:T(8,128)} custom-call(s32[32]{0:T(128)} %bitcast.13, s32[1,1,1]{2,1,0:T(1,128)S(6)} %copy.9.count_ref, bf16[1024,128]{1,0:T(8,128)(2,1)} %bitcast.8, bf16[2,1024]{1,0:T(2,128)(2,1)} %bitcast.11, s32[1,1024]{1,0:T(1,128)} %bitcast.12, f32[2,128,128]{2,1,0:T(8,128)} %bitcast.9, f32[128,128]{1,0:T(8,128)} %bitcast.10), custom_call_target="tpu_custom_call" | custom-call | tf_op jit(solution)/shard_map/pallas_call | solution.py:526
  63.5 1.6 %copy.10 = f32[1,2,128,128]{3,2,1,0:T(8,128)} copy(f32[1,2,128,128]{3,2,1,0:T(8,128)} %bitcast.7) | data formatting | bytes 262144

commit v5 on v4

--- a/solution.py
+++ b/solution.py
@@ -211,15 +211,19 @@
         ahead_z = (jnp.int32(code_z) >> (2 * turn)) & 3
         return lax.rem(y + ahead_y, ny) * nz + lax.rem(z + ahead_z, nz)
 
+    count_up = lax.broadcasted_iota(jnp.int32, (16, pts), 0)
+    levels = [(count_up + at).astype(jnp.float32).astype(jnp.bfloat16) for at in range(0, side, 16)]
+    one, zero = jnp.ones((16, pts), jnp.bfloat16), jnp.zeros((16, pts), jnp.bfloat16)
+
     def one_hots(turn, carry):
         tile = nearest(turn)
 
         vertex = idb[tile]
-        level = lax.broadcasted_iota(jnp.int32, (side, pts), 0)
-        pick_row = level == ((vertex - me * (side * side)) >> 7)
-        pick_col = level == (vertex & (side - 1))
-        row_hot = jnp.where(pick_row, 1.0, 0.0).astype(jnp.bfloat16)
-        col_hot = jnp.where(pick_col, 1.0, 0.0).astype(jnp.bfloat16)
+        hots = []
+        for place in ((vertex - me * (side * side)) >> 7, vertex & (side - 1)):
+            spread = jnp.broadcast_to(place.astype(jnp.float32), (16, pts)).astype(jnp.bfloat16)
+            hots.append(jnp.concatenate([jnp.where(level == spread, one, zero) for level in levels], axis=0))
+        row_hot, col_hot = hots
         onea[tile] = row_hot
         onec[tile] = col_hot
         mcount[...] += lax.dot_general(row_hot, col_hot, NT, preferred_element_type=jnp.float32)
@@ -490,12 +494,13 @@
                 out[channel] = moved
             else:
                 wire[turn, channel] = moved.astype(jnp.bfloat16)
-                for copy in swaps[turn + 1][4 + 2 * channel : 6 + 2 * channel]:
-                    copy.start()
+                if channel == 0:
+                    for copy in swaps[turn + 1][4:6]:
+                        copy.start()
                 ub[turn, channel] = moved
                 set_edges(turn + 1, channel, moved)
         if turn < ITERS - 1:
-            for copy in swaps[turn + 1][:4]:
+            for copy in swaps[turn + 1][:4] + swaps[turn + 1][6:]:
                 copy.start()
 
     for copy in shift + tables + names + queries + keys + partials + [c for swap in swaps for c in swap]:

time: 66 us -> 65.1 us (0.986)
  Pallas kernels: 62.8 us -> 61.9 us
    pallas_call x1, Pallas kernels: 62.8 us -> 61.9 us  [per_device(): pl.pallas_call(functools.partial(kernel, (ns, ny, nz, blocks.shape[0])),...]
where the time goes in v5:
time: 65.1 us; the launch traced here: 64.1 us
  Pallas kernels  61.9 us (95%)
  local copies, waits for them, and re-layouts  1.57 us (2%)
  between operations  0.66 us (1%)
    pallas_call x1, Pallas kernels, per_device(): pl.pallas_call(functools.partial(kernel, (ns, ny, nz, blocks.shape[0])),...  61.9 us
    unnamed x1, local copies, waits for them, and re-layouts  1.57 us

profile of v5, /device:TPU:4, one launch (start us, length us, event | category | flops | bytes accessed | tf_op | source)
XLA Modules:
  0.0 64.1 jit_solution(404763750288521391)
XLA Ops:
  0.7 61.9 %shard_map.73 = f32[2,128,128]{2,1,0:T(8,128)} custom-call(s32[32]{0:T(128)} %bitcast.13, s32[1,1,1]{2,1,0:T(1,128)S(6)} %copy.9.count_ref, bf16[1024,128]{1,0:T(8,128)(2,1)} %bitcast.8, bf16[2,1024]{1,0:T(2,128)(2,1)} %bitcast.11, s32[1,1024]{1,0:T(1,128)} %bitcast.12, f32[2,128,128]{2,1,0:T(8,128)} %bitcast.9, f32[128,128]{1,0:T(8,128)} %bitcast.10), custom_call_target="tpu_custom_call" | custom-call | tf_op jit(solution)/shard_map/pallas_call | solution.py:531
  62.6 1.6 %copy.10 = f32[1,2,128,128]{3,2,1,0:T(8,128)} copy(f32[1,2,128,128]{3,2,1,0:T(8,128)} %bitcast.7) | data formatting | bytes 262144
